TPU v7x, 32 devices: a whole 2x2x4 slice. The times are simulated.
32 devices in a mesh: dp: 2 (over x), cols: 16 (over z, y, core).
Axes of the slice: x: 2, y: 2, z: 4, core: 2. Of those that a mesh axis runs over, the one named last changes fastest.
Arguments:
- tokens: bfloat16 [512, 4096], P(('dp', 'cols')), may hold values from -6 to 6
- cotangent: bfloat16 [512, 4096], P(('dp', 'cols')), may hold values from -6 to 6
- block_weights: bfloat16 [4096, 128, 128], P('cols'), may hold values from -0.15625 to 0.15625
- slot_block: int32 [4096], P('cols'), may hold values from 0 to 31
- slot_target: int32 [4096], P('cols'), may hold values from 0 to 23, as said below
- counts: int32 [16], P('cols'), may hold values from 171 to 256, as said below
Outputs:
- input_grad: bfloat16 [512, 4096], P(('dp', 'cols'))
- weight_grad: bfloat16 [4096, 128, 128], P('cols', 'dp')
Inputs may be any that keep to these rules, and one draw needn't show every extreme that they name: On each device the live slots name distinct pairs of slot_target and slot_block; slot_target // 8 gives the matrix (0 gate, 1 up, 2 down). `counts`: some device has all 256 slots live.
All inputs are finite; a program needn't handle non-finite values.
Results may differ from a plain program's by a relative error of at most 0.018.
Values may be sent and summed in bfloat16 or wider, within the bound.
A program may use at most 192 MiB of HBM per device.

v0:
```python
import functools

import jax
import jax.numpy as jnp
from jax import lax
from jax.experimental import pallas as pl
from jax.experimental.pallas import tpu as pltpu
from jax.sharding import PartitionSpec as P

SPC = 32


def block_inputs(grad_rows, weights, block_select):
    partial_rows = jnp.einsum(
        "rsj,skj->rsk", grad_rows, weights, preferred_element_type=jnp.float32
    )
    summed = jnp.einsum("rsk,sb->rbk", partial_rows, block_select)
    return summed.reshape(summed.shape[0], summed.shape[1] * summed.shape[2])


def shards(tokens, cotangent, block_weights, slot_block, slot_target, counts):
    slot_total = block_weights.shape[0]
    block_width = block_weights.shape[1]
    columns = slot_total // SPC
    features = tokens.shape[1]
    block_count = features // block_width
    tokens_all, cot_all = (
        lax.all_gather(tokens, "cols", axis=0, tiled=True),
        lax.all_gather(cotangent, "cols", axis=0, tiled=True),
    )
    row_total = tokens_all.shape[0]
    live_slot = jnp.arange(slot_total) < counts[0]
    slot_kind = slot_target // columns
    places = slot_target % columns
    up_mask = (live_slot & (slot_kind < 2))[:, None].astype(jnp.float32)
    down_mask = (live_slot & (slot_kind == 2))[:, None].astype(jnp.float32)
    select_up = jax.nn.one_hot(slot_target, 2 * columns, dtype=jnp.float32) * up_mask
    select_down = jax.nn.one_hot(places, columns, dtype=jnp.float32) * down_mask
    block_select = jax.nn.one_hot(slot_block, block_count, dtype=jnp.float32)
    tokens_slots = jnp.take(
        tokens_all.reshape(row_total, block_count, block_width), slot_block, axis=1
    )
    products = jnp.einsum(
        "rsk,skj->rsj", tokens_slots, block_weights, preferred_element_type=jnp.float32
    )
    gate_up = jnp.einsum("rsj,sc->rcj", products, select_up)
    gate_pre = gate_up[:, :columns]
    up_pre = gate_up[:, columns:]
    sigmoid_gate = jax.nn.sigmoid(gate_pre)
    silu_gate = gate_pre * sigmoid_gate
    hidden = (silu_gate * up_pre).astype(jnp.bfloat16)
    cot_slots = jnp.take(cot_all.reshape(row_total, block_count, block_width), slot_block, axis=1)
    back_products = jnp.einsum(
        "rsj,skj->rsk", cot_slots, block_weights, preferred_element_type=jnp.float32
    )
    hidden_grad = jnp.einsum("rsk,sc->rck", back_products, select_down)
    gate_grad = (
        hidden_grad * up_pre * sigmoid_gate * (1.0 + gate_pre * (1.0 - sigmoid_gate))
    ).astype(jnp.bfloat16)
    up_grad = (hidden_grad * silu_gate).astype(jnp.bfloat16)
    pre_grad = jnp.concatenate([gate_grad, up_grad], axis=1)
    slot_grad = jnp.einsum(
        "rck,sc->rsk", pre_grad, select_up.astype(jnp.bfloat16), preferred_element_type=jnp.float32
    ).astype(jnp.bfloat16)
    slot_hidden = jnp.einsum(
        "rck,sc->rsk", hidden, select_down.astype(jnp.bfloat16), preferred_element_type=jnp.float32
    ).astype(jnp.bfloat16)
    weight_terms = jnp.einsum(
        "rsk,rsj->skj", tokens_slots, slot_grad, preferred_element_type=jnp.float32
    )
    weight_terms = weight_terms + jnp.einsum(
        "rsk,rsj->skj", slot_hidden, cot_slots, preferred_element_type=jnp.float32
    )
    input_terms = block_inputs(slot_grad, block_weights, block_select)
    input_sum = lax.psum_scatter(input_terms, "cols", scatter_dimension=0, tiled=True)
    input_grad = input_sum.astype(jnp.bfloat16)
    weight_sum = lax.psum_scatter(
        weight_terms.astype(jnp.bfloat16), "dp", scatter_dimension=1, tiled=True
    )
    return (input_grad, weight_sum)


MESH = pl.DeviceIdType.MESH
F32 = jnp.float32
BF16 = jnp.bfloat16
NT = (((1,), (1,)), ((), ()))
CHUNKS = 4


def layer_kernel(
    n_cols, table_ref, slots_ref, tok_ref, cot_ref, w_ref, in_ref, wg_ref,
    tok, cot, blocks, wgu, wd, grads, hid, pre, acc, sib_out, sib_in, chip_sum, a2a,
    fin_out, fin_in, lhs, hid_t,
    w_sem, own_sem, ring_send, ring_recv, sib_send, sib_recv,
    x_send, x_recv, half_send, half_recv, a2a_send, a2a_recv, fin_send, fin_recv,
):
    chips = n_cols // 2
    steps = chips // 2
    rows = tok_ref.shape[0]
    group_rows = rows * n_cols
    features = tok_ref.shape[1]
    width = blocks.shape[2]
    part = blocks.shape[1]
    n_f = features // width
    hidden = wd.shape[0]
    n_h = hidden // width
    zero_at = blocks.shape[0] - 1
    half = features // 2
    dp = lax.axis_index("dp")
    col = lax.axis_index("cols")
    core = col % 2
    chip = col // 2
    place = jnp.where(chip % 2 == 0, chip // 2, chips - 1 - chip // 2)

    def chip_at(p):
        p = (p + 2 * chips) % chips
        return jnp.where(p < steps, 2 * p, 2 * (chips - 1 - p) + 1)

    right = chip_at(place + 1) * 2 + core
    left = chip_at(place - 1) * 2 + core
    sibling = chip * 2 + 1 - core
    sides = ((tok_ref, tok), (cot_ref, cot))

    owns = [pltpu.make_async_copy(sides[a][0], sides[a][1].at[0, col], own_sem.at[a]) for a in range(2)]
    for own in owns:
        own.start()
    w_copy = pltpu.make_async_copy(w_ref, blocks.at[pl.ds(0, w_ref.shape[0])], w_sem)
    w_copy.start()
    barrier = pltpu.get_barrier_semaphore()
    for r in range(1, chips):
        pl.semaphore_signal(barrier, inc=1, device_id=(dp, ((chip + r) % chips) * 2 + core), device_id_type=MESH)
    pl.semaphore_signal(barrier, inc=1, device_id=(dp, sibling), device_id_type=MESH)
    pl.semaphore_signal(barrier, inc=1, device_id=(1 - dp, col), device_id_type=MESH)
    pl.semaphore_wait(barrier, chips + 1)

    def piece(g, origin, a):
        at = pl.ds((a % 2) * half, half)
        return sides[a // 2][1].at[g, origin * 2 + core, :, at]

    def ring_copy(g, origin, direction, s, a):
        block = piece(g, origin, a)
        return pltpu.make_async_remote_copy(
            src_ref=block, dst_ref=block,
            send_sem=ring_send.at[g, direction, s, a], recv_sem=ring_recv.at[g, direction, s, a],
            device_id=(dp, right if direction == 0 else left), device_id_type=MESH,
        )

    def ring(g, direction, s, a):
        return ring_copy(g, chip_at(place - s if direction == 0 else place + s), direction, s, a)

    def ring_arrival(g, direction, s, a):
        return ring_copy(g, chip_at(place - 1 - s if direction == 0 else place + 1 + s), direction, s, a)

    def share_copy(g, k, a, lane):
        at = pl.ds((a % 2) * half, half)
        block = sides[a // 2][1].at[g, chip_at(place - k) * 2 + lane, :, at]
        return pltpu.make_async_remote_copy(
            src_ref=block, dst_ref=block,
            send_sem=sib_send.at[g, k, a], recv_sem=sib_recv.at[g, k, a],
            device_id=(dp, sibling), device_id_type=MESH,
        )

    def share(g, k, a):
        return share_copy(g, k, a, core)

    def cross(k, a):
        origin = chip_at(place - k)
        return pltpu.make_async_remote_copy(
            src_ref=piece(0, origin, a), dst_ref=piece(1, origin, a),
            send_sem=x_send.at[k, a], recv_sem=x_recv.at[k, a],
            device_id=(1 - dp, col), device_id_type=MESH,
        )

    def first(g, arr):
        for a in (2 * arr, 2 * arr + 1):
            for direction in range(2):
                ring(g, direction, 0, a).start()
        for a in (2 * arr, 2 * arr + 1):
            share(g, 0, a).start()
            if g == 0:
                cross(0, a).start()

    def pass_on(s, direction, a):
        ring_arrival(0, direction, s, a).wait_recv()

        far = steps - 1 if a % 2 == direction else steps - 2

        @pl.when(s < far)
        def _():
            ring(0, direction, s + 1, a).start()

        k = 1 + s if direction == 0 else chips - 1 - s
        share(0, k, a).start()

        @pl.when(s > 0)
        def _():
            cross(k, a).start()

    def advance(s, arr):
        for direction in range(2):
            pass_on(s, direction, 2 * arr + direction)

        @pl.when(s < steps - 1)
        def _():
            for direction in range(2):
                pass_on(s, direction, 2 * arr + 1 - direction)

    def all_shared(g, arr):
        @pl.loop(0, chips)
        def _(k):
            for a in (2 * arr, 2 * arr + 1):
                share_copy(g, k, a, 1 - core).wait_recv()

    def crossed(k):
        for a in range(4):
            cross(k, a).wait_recv()
            share(1, k, a).start()

    for own in owns:
        own.wait()
    first(0, 0)
    blocks[zero_at] = jnp.zeros((part, width), BF16)
    w_copy.wait()

    pieces = width // part

    def spread(h, f):
        at = pl.multiple_of(f * width, width)
        hid_at = pl.multiple_of(h * width, width)
        for k in range(3):
            index = table_ref[(k * n_h + h) * n_f + f]
            for piece in range(pieces):
                value = blocks[jnp.minimum(index * pieces + piece, zero_at)]
                if k < 2:
                    wgu[pl.ds(pl.multiple_of(at + piece * part, part), part),
                        pl.ds(pl.multiple_of(k * hidden + hid_at, width), width)] = value
                else:
                    wd[pl.ds(pl.multiple_of(hid_at + piece * part, part), part), pl.ds(at, width)] = value

    per_step = n_h // steps

    @pl.loop(0, steps)
    def _(s):
        @pl.loop(0, n_f)
        def _(f):
            for j in range(per_step):
                spread(s * per_step + j, f)

        advance(s, 0)

        @pl.when(s == steps // 2 - 1)
        def _():
            first(0, 1)

    all_shared(0, 0)
    span = hidden // steps

    def before(g, n):
        at = pl.multiple_of(n * span, span)
        x = tok[g].reshape(group_rows, features)
        gate = jnp.dot(x, wgu[:, pl.ds(at, span)], preferred_element_type=F32)
        up = jnp.dot(x, wgu[:, pl.ds(pl.multiple_of(hidden + at, span), span)], preferred_element_type=F32)
        return gate, up

    def after(g, n, gate, up):
        at = pl.multiple_of(n * span, span)
        back = lax.dot_general(
            cot[g].reshape(group_rows, features), wd[pl.ds(at, span), :], NT, preferred_element_type=F32
        )
        sig = jax.nn.sigmoid(gate)
        silu = gate * sig
        hid[g, :, pl.ds(at, span)] = (silu * up).astype(BF16)
        grads[g, :, pl.ds(at, span)] = (back * up * sig * (1.0 + gate * (1.0 - sig))).astype(BF16)
        grads[g, :, pl.ds(pl.multiple_of(hidden + at, span), span)] = (back * silu).astype(BF16)

    @pl.loop(0, steps)
    def _(s):
        gate, up = before(0, s)
        pre[s, 0] = gate
        pre[s, 1] = up
        advance(s, 1)

    for a in range(4):
        cross(0, a).wait_recv()
    first(1, 0)
    first(1, 1)
    all_shared(0, 1)

    @pl.loop(0, steps)
    def _(s):
        after(0, s, pre[s, 0], pre[s, 1])

    crossed(2)
    crossed(chips - 2)

    chunk = half // CHUNKS
    chip_rows = group_rows // chips

    def terms(at):
        return lax.dot_general(grads[0], wgu[pl.ds(at, chunk), :], NT, preferred_element_type=F32)

    def to_sibling(i):
        return pltpu.make_async_remote_copy(
            src_ref=sib_out.at[i], dst_ref=sib_in.at[i], send_sem=half_send.at[i], recv_sem=half_recv.at[i],
            device_id=(dp, sibling), device_id_type=MESH,
        )

    def spread_sum(r, i):
        other = (chip + r) % chips
        return pltpu.make_async_remote_copy(
            src_ref=chip_sum.at[i, other], dst_ref=a2a.at[i, r],
            send_sem=a2a_send.at[i, r], recv_sem=a2a_recv.at[i, r],
            device_id=(dp, other * 2 + core), device_id_type=MESH,
        )

    def pair_sum(i):
        to_sibling(i).wait_recv()

        @pl.loop(0, chips)
        def _(c):
            at = pl.ds(pl.multiple_of(c * chip_rows, chip_rows), chip_rows)
            total = acc[i, at, :] + sib_in[i, at, :].astype(F32)
            acc[i, at, :] = total
            chip_sum[i, c] = total.astype(BF16)

        @pl.loop(1, chips)
        def _(r):
            spread_sum(r, i).start()

    @pl.loop(0, CHUNKS)
    def _(i):
        at = pl.multiple_of(i * chunk, chunk)
        sib_out[i] = terms(pl.multiple_of((1 - core) * half + at, chunk)).astype(BF16)
        to_sibling(i).start()
        acc[i] = terms(pl.multiple_of(core * half + at, chunk))

        @pl.when(i > 0)
        def _():
            pair_sum(i - 1)

    pair_sum(CHUNKS - 1)

    for direction in range(2):
        for a in range(4):
            ring_arrival(1, direction, 0, a).wait_recv()
            share(1, 1 if direction == 0 else chips - 1, a).start()

    @pl.loop(3, chips - 2)
    def _(k):
        crossed(k)

    all_shared(1, 0)
    all_shared(1, 1)

    @pl.loop(0, steps)
    def _(s):
        gate, up = before(1, s)
        after(1, s, gate, up)

    def take_part(block):
        out = block[:part]
        for i in range(1, width // part):
            out = jnp.where(dp == i, block[i * part:(i + 1) * part], out)
        return out

    for g in range(2):
        for h in range(n_h):
            hid_t[pl.ds(h * part, part), pl.ds(g * group_rows, group_rows)] = take_part(
                hid[g, :, pl.ds(h * width, width)].T
            )
    four = 4

    @pl.loop(0, n_f // four)
    def _(i):
        at = pl.multiple_of(i * four * width, four * width)
        for g in range(2):
            for b in range(four):
                piece = tok[g, :, :, pl.ds(pl.multiple_of(at + b * width, width), width)]
                lhs[pl.ds(b * part, part), pl.ds(g * group_rows, group_rows)] = take_part(
                    piece.reshape(group_rows, width).T
                )
        for n in range(2 * n_h // 4):
            cut = slice(n * 4 * width, (n + 1) * 4 * width)
            out = jnp.dot(
                lhs[...], grads[:, :, cut].reshape(2 * group_rows, 4 * width), preferred_element_type=F32
            ).astype(BF16)
            for h in range(4):
                for b in range(four):
                    blocks[(n * 4 + h) * n_f + i * four + b] = out[
                        b * part:(b + 1) * part, h * width:(h + 1) * width
                    ]
        c = cot[:, :, :, pl.ds(at, four * width)].reshape(2 * group_rows, four * width)
        out = jnp.dot(hid_t[...], c, preferred_element_type=F32).astype(BF16)
        for h in range(n_h):
            for b in range(four):
                blocks[(2 * n_h + h) * n_f + i * four + b] = out[
                    h * part:(h + 1) * part, b * width:(b + 1) * width
                ]

    @pl.loop(0, wg_ref.shape[0], unroll=8)
    def _(s):
        wg_ref[s] = blocks[slots_ref[s]]

    mine = pl.ds(pl.multiple_of(chip * chip_rows, chip_rows), chip_rows)

    @pl.loop(0, CHUNKS)
    def _(i):
        total = acc[i, mine, :]
        for r in range(1, chips):
            spread_sum(r, i).wait_recv()
            total = total + a2a[i, r].astype(F32)
        low, high = total[:rows], total[rows:]
        at = pl.multiple_of(i * chunk, chunk)
        fin_out[:, pl.ds(at, chunk)] = jnp.where(core == 0, high, low)
        in_ref[:, pl.ds(pl.multiple_of(core * half + at, chunk), chunk)] = jnp.where(core == 0, low, high)

    fin = pltpu.make_async_remote_copy(
        src_ref=fin_out, dst_ref=fin_in, send_sem=fin_send, recv_sem=fin_recv,
        device_id=(dp, sibling), device_id_type=MESH,
    )
    fin.start()

    @pl.loop(0, CHUNKS)
    def _(i):
        to_sibling(i).wait_send()

        @pl.loop(1, chips)
        def _(r):
            spread_sum(r, i).wait_send()

    for a in range(4):
        @pl.loop(0, chips)
        def _(k):
            share(0, k, a).wait_send()
            share(1, k, a).wait_send()

        cross(0, a).wait_send()

        @pl.loop(2, chips - 1)
        def _(k):
            cross(k, a).wait_send()

        for direction in range(2):
            @pl.loop(0, steps if a % 2 == direction else steps - 1)
            def _(s):
                ring(0, direction, s, a).wait_send()

            ring(1, direction, 0, a).wait_send()

    fin.wait()
    in_ref[:, pl.ds(pl.multiple_of((1 - core) * half, half), half)] = fin_in[...]


def kernel_shards(n_cols, tokens, cotangent, block_weights, slot_block, slot_target, counts):
    n_slots, width = block_weights.shape[:2]
    n_dp = 2
    part = width // n_dp
    rows, features = tokens.shape
    n_f = features // width
    hidden_blocks = n_slots // SPC
    hidden = hidden_blocks * width
    places = 3 * hidden_blocks * n_f
    place = slot_target * n_f + slot_block
    number = jnp.arange(n_slots, dtype=jnp.int32)
    live = number < counts[0]
    hit = (place[None, :] == jnp.arange(places, dtype=jnp.int32)[:, None]) & live[None, :]
    table = places + jnp.sum(jnp.where(hit, number[None, :] - places, 0), axis=1)
    slots = jnp.where(live, place, 0)
    chips = n_cols // 2
    group_rows = rows * n_cols
    half = features // 2
    dma = pltpu.SemaphoreType.DMA
    vmem = pl.BlockSpec(memory_space=pltpu.VMEM)
    smem = pl.BlockSpec(memory_space=pltpu.SMEM)
    input_sum, weight_sum = pl.pallas_call(
        functools.partial(layer_kernel, n_cols),
        out_shape=(
            jax.ShapeDtypeStruct((rows, features), F32),
            jax.ShapeDtypeStruct((n_slots, part, width), BF16),
        ),
        in_specs=[smem, smem, vmem, vmem, pl.BlockSpec(memory_space=pl.ANY)],
        out_specs=(vmem, vmem),
        scratch_shapes=[
            pltpu.VMEM((n_dp, n_cols, rows, features), BF16),
            pltpu.VMEM((n_dp, n_cols, rows, features), BF16),
            pltpu.VMEM((places + 1, part, width), BF16),
            pltpu.VMEM((features, 2 * hidden), BF16),
            pltpu.VMEM((hidden, features), BF16),
            pltpu.VMEM((n_dp, group_rows, 2 * hidden), BF16),
            pltpu.VMEM((n_dp, group_rows, hidden), BF16),
            pltpu.VMEM((chips // 2, 2, group_rows, hidden // (chips // 2)), F32),
            pltpu.VMEM((CHUNKS, group_rows, half // CHUNKS), F32),
            pltpu.VMEM((CHUNKS, group_rows, half // CHUNKS), BF16),
            pltpu.VMEM((CHUNKS, group_rows, half // CHUNKS), BF16),
            pltpu.VMEM((CHUNKS, chips, group_rows // chips, half // CHUNKS), BF16),
            pltpu.VMEM((CHUNKS, chips, group_rows // chips, half // CHUNKS), BF16),
            pltpu.VMEM((rows, half), F32),
            pltpu.VMEM((rows, half), F32),
            pltpu.VMEM((4 * part, n_dp * group_rows), BF16),
            pltpu.VMEM((hidden // n_dp, n_dp * group_rows), BF16),
            dma, dma((2,)),
            dma((2, 2, chips // 2, 4)), dma((2, 2, chips // 2, 4)),
            dma((2, chips, 4)), dma((2, chips, 4)),
            dma((chips, 4)), dma((chips, 4)), dma((CHUNKS,)), dma((CHUNKS,)),
            dma((CHUNKS, chips)), dma((CHUNKS, chips)), dma, dma,
        ],
        compiler_params=pltpu.CompilerParams(
            collective_id=0, has_side_effects=True, vmem_limit_bytes=67043328
        ),
    )(table, slots, tokens, cotangent, block_weights.reshape(n_slots * n_dp, part, width))
    weight_grad = jnp.where(live[:, None, None], weight_sum, jnp.zeros((), BF16))
    return (input_sum.astype(BF16), weight_grad)


def solution(mesh):
    n_dp, n_cols = mesh.shape["dp"], mesh.shape["cols"]
    paired = n_dp == 2 and n_cols % 4 == 0

    def body(*args):
        tokens, weights = args[0], args[2]
        if paired and tokens.shape[0] % 16 == 0 and weights.shape[0] // SPC % (n_cols // 4) == 0:
            return kernel_shards(n_cols, *args)
        return shards(*args)

    return jax.shard_map(
        body,
        mesh=mesh,
        in_specs=(
            P(("dp", "cols"), None),
            P(("dp", "cols"), None),
            P("cols", None, None),
            P("cols"),
            P("cols"),
            P("cols"),
        ),
        out_specs=(P(("dp", "cols"), None), P("cols", "dp", None)),
        check_vma=False,
    )
```

profile of v0, /device:TPU:0, one launch (start us, length us, event | category | flops | bytes accessed | tf_op | source)
XLA Modules:
  0.0 81.3 jit_solution(2344352274056538426)
XLA Ops:
  1.3 0.0 copy-start
  1.3 1.3 %broadcast_select_fusion.1 = (s32[256]{0:T(256)}, s32[256]{0:T(256)S(1)}, s32[256]{0:T(256)S(1)}) fusion(s32[]{:T(128)} %bitcast.3, s32[256]{0:T(256)} %param.9, s32[256]{0:T(256)} %param.10), kind=kLoop, calls=%fused_computation.8 | loop fusion | flops 1280 | bytes 5124 | tf_op jit(solution)/shard_map/jit(_where)/select_n | solution.py:468
  2.6 0.2 select_reduce_fusion
  2.8 0.0 copy-done
  2.8 0.6 broadcast_add_fusion.table_ref
  3.4 72.2 %shard_map.77 = (f32[16,4096]{1,0:T(8,128)}, bf16[256,64,128]{2,1,0:T(8,128)(2,1)}) custom-call(s32[768]{0:T(1024)} %broadcast_add_fusion.table_ref, s32[256]{0:T(256)} %get-tuple-element.6.slots_ref, bf16[16,4096]{1,0:T(8,128)(2,1)} %tok_ref.1, bf16[16,4096]{1,0:T(8,128)(2,1)} %cot_ref.1, bf16[512,64,128]{2,1,0:T(8,128)(2,1)} %bitcast.4), custom_call_target="tpu_custom_call" | custom-call | tf_op jit(solution)/shard_map/pallas_call | solution.py:475
  75.6 1.6 %convert_element_type.3 = bf16[16,4096]{1,0:T(8,128)(2,1)} convert(f32[16,4096]{1,0:T(8,128)} %get-tuple-element.4) | non-fusion elementwise | flops 65536 | bytes 393216 | tf_op jit(solution)/shard_map/convert_element_type | solution.py:512
  77.3 4.0 %broadcast_select_fusion = bf16[256,64,128]{2,1,0:T(8,128)(2,1)} fusion(bf16[256,64,128]{2,1,0:T(8,128)(2,1)} %get-tuple-element.5, pred[256]{0:T(512)(128)(4,1)} %copy-done), kind=kLoop, calls=%fused_computation | loop fusion | flops 2097152 | bytes 8388864 | tf_op jit(solution)/shard_map/jit(_where)/select_n | solution.py:511
  (1 shorter events, 0.0 us)
Async XLA Ops:
  1.3 1.5 %copy-start = (pred[256]{0:T(512)(128)(4,1)}, pred[256]{0:T(512)(128)(4,1)S(1)}, u32[]{:S(2)}) copy-start(pred[256]{0:T(512)(128)(4,1)S(1)} %iota_compare_fusion.1) | copy-start | bytes 772
where the time goes:
time: 81.5 us; the launch traced here: 81.3 us
  Pallas kernels  72.2 us (89%)
  other arithmetic  7.71 us (9%)
  between operations  1.31 us (2%)
    pallas_call x1, Pallas kernels, kernel_shards(): pl.pallas_call(functools.partial(layer_kernel, n_cols), out_shape=(jax.Sh...  72.2 us
    select_n x1, other arithmetic, kernel_shards(): jnp.where(live[:, None, None], weight_sum, jnp.zeros((), BF16))  3.99 us

commit v1 on v0

--- a/solution.py
+++ b/solution.py
@@ -85,13 +85,15 @@
 BF16 = jnp.bfloat16
 NT = (((1,), (1,)), ((), ()))
 CHUNKS = 4
+GROUP = 4
+LANES = 128
 
 
 def layer_kernel(
-    n_cols, table_ref, slots_ref, tok_ref, cot_ref, w_ref, in_ref, wg_ref,
+    n_cols, count_ref, target_ref, block_ref, tok_ref, cot_ref, w_ref, in_ref, out_ref,
     tok, cot, blocks, wgu, wd, grads, hid, pre, acc, sib_out, sib_in, chip_sum, a2a,
-    fin_out, fin_in, lhs, hid_t,
-    w_sem, own_sem, ring_send, ring_recv, sib_send, sib_recv,
+    fin_out, fin_in, lhs, hid_t, table_rows, table_ref,
+    w_sem, own_sem, table_sem, out_sem, ring_send, ring_recv, sib_send, sib_recv,
     x_send, x_recv, half_send, half_recv, a2a_send, a2a_recv, fin_send, fin_recv,
 ):
     chips = n_cols // 2
@@ -105,6 +107,7 @@
     hidden = wd.shape[0]
     n_h = hidden // width
     zero_at = blocks.shape[0] - 1
+    zero_slot = zero_at
     half = features // 2
     dp = lax.axis_index("dp")
     col = lax.axis_index("cols")
@@ -141,7 +144,7 @@
         block = piece(g, origin, a)
         return pltpu.make_async_remote_copy(
             src_ref=block, dst_ref=block,
-            send_sem=ring_send.at[g, direction, s, a], recv_sem=ring_recv.at[g, direction, s, a],
+            send_sem=ring_send, recv_sem=ring_recv.at[g * steps + s, direction, a],
             device_id=(dp, right if direction == 0 else left), device_id_type=MESH,
         )
 
@@ -156,7 +159,7 @@
         block = sides[a // 2][1].at[g, chip_at(place - k) * 2 + lane, :, at]
         return pltpu.make_async_remote_copy(
             src_ref=block, dst_ref=block,
-            send_sem=sib_send.at[g, k, a], recv_sem=sib_recv.at[g, k, a],
+            send_sem=sib_send, recv_sem=sib_recv.at[g, a // 2],
             device_id=(dp, sibling), device_id_type=MESH,
         )
 
@@ -167,7 +170,7 @@
         origin = chip_at(place - k)
         return pltpu.make_async_remote_copy(
             src_ref=piece(0, origin, a), dst_ref=piece(1, origin, a),
-            send_sem=x_send.at[k, a], recv_sem=x_recv.at[k, a],
+            send_sem=x_send, recv_sem=x_recv.at[k],
             device_id=(1 - dp, col), device_id_type=MESH,
         )
 
@@ -205,22 +208,50 @@
             for direction in range(2):
                 pass_on(s, direction, 2 * arr + 1 - direction)
 
+    def bulk(ref, send_sem, recv_sem, device):
+        return pltpu.make_async_remote_copy(
+            src_ref=ref, dst_ref=ref, send_sem=send_sem, recv_sem=recv_sem,
+            device_id=device, device_id_type=MESH,
+        )
+
     def all_shared(g, arr):
-        @pl.loop(0, chips)
-        def _(k):
-            for a in (2 * arr, 2 * arr + 1):
-                share_copy(g, k, a, 1 - core).wait_recv()
+        bulk(sides[arr][1].at[g, pl.ds(0, chips)], sib_send, sib_recv.at[g, arr], (dp, sibling)).wait_recv()
+
+    def cross_arrival(k):
+        bulk(tok.at[1, pl.ds(0, 2)], x_send, x_recv.at[k], (1 - dp, col)).wait_recv()
 
     def crossed(k):
+        cross_arrival(k)
         for a in range(4):
-            cross(k, a).wait_recv()
             share(1, k, a).start()
 
     for own in owns:
         own.wait()
     first(0, 0)
+
+    slot_place = target_ref[...] * n_f + block_ref[...]
+    number = lax.broadcasted_iota(jnp.int32, slot_place.shape, 0) * LANES + lax.broadcasted_iota(
+        jnp.int32, slot_place.shape, 1
+    )
+    slot_place = jnp.where(number < count_ref[0], slot_place, -1)
+    lane = lax.broadcasted_iota(jnp.int32, (LANES, LANES), 1)
+    in_row = lax.broadcasted_iota(jnp.int32, (LANES, LANES), 0)
+    columns = [
+        jnp.broadcast_to(slot_place[j:j + 1], (LANES, LANES)).T for j in range(slot_place.shape[0])
+    ]
+    for t in range(zero_slot // LANES):
+        row = jnp.zeros((1, LANES), jnp.int32)
+        for j, column in enumerate(columns):
+            hit = column == lane + t * LANES
+            row = row + jnp.sum(
+                jnp.where(hit, in_row + (j * LANES - zero_slot), 0), axis=0, keepdims=True
+            )
+        table_rows[t:t + 1, :] = row + zero_slot
+    table_copy = pltpu.make_async_copy(table_rows, table_ref, table_sem)
+    table_copy.start()
     blocks[zero_at] = jnp.zeros((part, width), BF16)
     w_copy.wait()
+    table_copy.wait()
 
     pieces = width // part
 
@@ -228,7 +259,8 @@
         at = pl.multiple_of(f * width, width)
         hid_at = pl.multiple_of(h * width, width)
         for k in range(3):
-            index = table_ref[(k * n_h + h) * n_f + f]
+            entry = (k * n_h + h) * n_f + f
+            index = table_ref[entry // LANES, entry % LANES]
             for piece in range(pieces):
                 value = blocks[jnp.minimum(index * pieces + piece, zero_at)]
                 if k < 2:
@@ -280,8 +312,7 @@
         pre[s, 1] = up
         advance(s, 1)
 
-    for a in range(4):
-        cross(0, a).wait_recv()
+    cross_arrival(0)
     first(1, 0)
     first(1, 1)
     all_shared(0, 1)
@@ -301,7 +332,7 @@
 
     def to_sibling(i):
         return pltpu.make_async_remote_copy(
-            src_ref=sib_out.at[i], dst_ref=sib_in.at[i], send_sem=half_send.at[i], recv_sem=half_recv.at[i],
+            src_ref=sib_out.at[i], dst_ref=sib_in.at[i], send_sem=half_send, recv_sem=half_recv.at[i],
             device_id=(dp, sibling), device_id_type=MESH,
         )
 
@@ -309,7 +340,7 @@
         other = (chip + r) % chips
         return pltpu.make_async_remote_copy(
             src_ref=chip_sum.at[i, other], dst_ref=a2a.at[i, r],
-            send_sem=a2a_send.at[i, r], recv_sem=a2a_recv.at[i, r],
+            send_sem=a2a_send, recv_sem=a2a_recv.at[i],
             device_id=(dp, other * 2 + core), device_id_type=MESH,
         )
 
@@ -368,7 +399,16 @@
             hid_t[pl.ds(h * part, part), pl.ds(g * group_rows, group_rows)] = take_part(
                 hid[g, :, pl.ds(h * width, width)].T
             )
-    four = 4
+    four = GROUP
+    per_piece = 3 * n_h * four
+    cuts = 4
+
+    def send_out(i, c):
+        at = pl.ds(i * per_piece + c * (per_piece // cuts), per_piece // cuts)
+        return pltpu.make_async_copy(blocks.at[at], out_ref.at[at], out_sem)
+
+    zero_out = pltpu.make_async_copy(blocks.at[zero_at], out_ref.at[zero_at], table_sem)
+    zero_out.start()
 
     @pl.loop(0, n_f // four)
     def _(i):
@@ -379,6 +419,7 @@
                 lhs[pl.ds(b * part, part), pl.ds(g * group_rows, group_rows)] = take_part(
                     piece.reshape(group_rows, width).T
                 )
+        base = i * per_piece
         for n in range(2 * n_h // 4):
             cut = slice(n * 4 * width, (n + 1) * 4 * width)
             out = jnp.dot(
@@ -386,28 +427,26 @@
             ).astype(BF16)
             for h in range(4):
                 for b in range(four):
-                    blocks[(n * 4 + h) * n_f + i * four + b] = out[
+                    blocks[base + (n * 4 + h) * four + b] = out[
                         b * part:(b + 1) * part, h * width:(h + 1) * width
                     ]
         c = cot[:, :, :, pl.ds(at, four * width)].reshape(2 * group_rows, four * width)
         out = jnp.dot(hid_t[...], c, preferred_element_type=F32).astype(BF16)
         for h in range(n_h):
             for b in range(four):
-                blocks[(2 * n_h + h) * n_f + i * four + b] = out[
+                blocks[base + (2 * n_h + h) * four + b] = out[
                     h * part:(h + 1) * part, b * width:(b + 1) * width
                 ]
-
-    @pl.loop(0, wg_ref.shape[0], unroll=8)
-    def _(s):
-        wg_ref[s] = blocks[slots_ref[s]]
+        for c in range(cuts):
+            send_out(i, c).start()
 
     mine = pl.ds(pl.multiple_of(chip * chip_rows, chip_rows), chip_rows)
 
     @pl.loop(0, CHUNKS)
     def _(i):
         total = acc[i, mine, :]
+        bulk(a2a.at[i, pl.ds(1, chips - 1)], a2a_send, a2a_recv.at[i], (dp, sibling)).wait_recv()
         for r in range(1, chips):
-            spread_sum(r, i).wait_recv()
             total = total + a2a[i, r].astype(F32)
         low, high = total[:rows], total[rows:]
         at = pl.multiple_of(i * chunk, chunk)
@@ -420,35 +459,55 @@
     )
     fin.start()
 
-    @pl.loop(0, CHUNKS)
-    def _(i):
-        to_sibling(i).wait_send()
-
-        @pl.loop(1, chips)
-        def _(r):
-            spread_sum(r, i).wait_send()
-
-    for a in range(4):
-        @pl.loop(0, chips)
-        def _(k):
-            share(0, k, a).wait_send()
-            share(1, k, a).wait_send()
-
-        cross(0, a).wait_send()
-
-        @pl.loop(2, chips - 1)
-        def _(k):
-            cross(k, a).wait_send()
-
-        for direction in range(2):
-            @pl.loop(0, steps if a % 2 == direction else steps - 1)
-            def _(s):
-                ring(0, direction, s, a).wait_send()
-
-            ring(1, direction, 0, a).wait_send()
+    bulk(sib_out, half_send, half_recv.at[0], (dp, sibling)).wait_send()
+    bulk(chip_sum.at[:, pl.ds(1, chips - 1)], a2a_send, a2a_recv.at[0], (dp, sibling)).wait_send()
+    bulk(tok, sib_send, sib_recv.at[0, 0], (dp, sibling)).wait_send()
+    bulk(tok.at[0, pl.ds(0, 2 * (chips - 2))], x_send, x_recv.at[0], (1 - dp, col)).wait_send()
+    bulk(tok.at[:, pl.ds(0, chips + 1)], ring_send, ring_recv.at[0, 0, 0], (dp, right)).wait_send()
+    zero_out.wait()
+    all_out = pl.ds(0, zero_at)
+    pltpu.make_async_copy(blocks.at[all_out], out_ref.at[all_out], out_sem).wait()
 
     fin.wait()
     in_ref[:, pl.ds(pl.multiple_of((1 - core) * half, half), half)] = fin_in[...]
+
+
+def gather_kernel(
+    count_ref, target_ref, block_ref, sum_ref, blocks_ref, in_ref, wg_ref, buf, in_sem, out_sem
+):
+    n_slots = wg_ref.shape[0]
+    chunks = in_sem.shape[0]
+    per_chunk = n_slots // chunks
+    zero_at = blocks_ref.shape[0] - 1
+    targets = 3 * (n_slots // SPC)
+    per_piece = targets * GROUP
+    count = count_ref[0]
+
+    @pl.loop(0, chunks)
+    def _(c):
+        for j in range(per_chunk):
+            s = c * per_chunk + j
+            f = block_ref[s]
+            at = (f // GROUP) * per_piece + target_ref[s] * GROUP + f % GROUP
+            pltpu.make_async_copy(
+                blocks_ref.at[jnp.where(s < count, at, zero_at)], buf.at[s], in_sem.at[c]
+            ).start()
+
+    in_ref[...] = sum_ref[...].astype(BF16)
+
+    def out(c):
+        at = pl.ds(c * per_chunk, per_chunk)
+        return pltpu.make_async_copy(buf.at[at], wg_ref.at[at], out_sem.at[c])
+
+    @pl.loop(0, chunks)
+    def _(c):
+        at = pl.ds(c * per_chunk, per_chunk)
+        pltpu.make_async_copy(blocks_ref.at[pl.ds(0, per_chunk)], buf.at[at], in_sem.at[c]).wait()
+        out(c).start()
+
+    @pl.loop(0, chunks)
+    def _(c):
+        out(c).wait()
 
 
 def kernel_shards(n_cols, tokens, cotangent, block_weights, slot_block, slot_target, counts):
@@ -460,26 +519,23 @@
     hidden_blocks = n_slots // SPC
     hidden = hidden_blocks * width
     places = 3 * hidden_blocks * n_f
-    place = slot_target * n_f + slot_block
-    number = jnp.arange(n_slots, dtype=jnp.int32)
-    live = number < counts[0]
-    hit = (place[None, :] == jnp.arange(places, dtype=jnp.int32)[:, None]) & live[None, :]
-    table = places + jnp.sum(jnp.where(hit, number[None, :] - places, 0), axis=1)
-    slots = jnp.where(live, place, 0)
     chips = n_cols // 2
     group_rows = rows * n_cols
     half = features // 2
     dma = pltpu.SemaphoreType.DMA
     vmem = pl.BlockSpec(memory_space=pltpu.VMEM)
     smem = pl.BlockSpec(memory_space=pltpu.SMEM)
-    input_sum, weight_sum = pl.pallas_call(
+    hbm = pl.BlockSpec(memory_space=pl.ANY)
+    table_shape = (places // LANES, LANES)
+    slot_rows = (n_slots // LANES, LANES)
+    input_sum, grad_blocks = pl.pallas_call(
         functools.partial(layer_kernel, n_cols),
         out_shape=(
             jax.ShapeDtypeStruct((rows, features), F32),
-            jax.ShapeDtypeStruct((n_slots, part, width), BF16),
+            jax.ShapeDtypeStruct((places + 1, part, width), BF16),
         ),
-        in_specs=[smem, smem, vmem, vmem, pl.BlockSpec(memory_space=pl.ANY)],
-        out_specs=(vmem, vmem),
+        in_specs=[smem, vmem, vmem, hbm, hbm, hbm],
+        out_specs=(vmem, hbm),
         scratch_shapes=[
             pltpu.VMEM((n_dp, n_cols, rows, features), BF16),
             pltpu.VMEM((n_dp, n_cols, rows, features), BF16),
@@ -498,18 +554,34 @@
             pltpu.VMEM((rows, half), F32),
             pltpu.VMEM((4 * part, n_dp * group_rows), BF16),
             pltpu.VMEM((hidden // n_dp, n_dp * group_rows), BF16),
-            dma, dma((2,)),
-            dma((2, 2, chips // 2, 4)), dma((2, 2, chips // 2, 4)),
-            dma((2, chips, 4)), dma((2, chips, 4)),
-            dma((chips, 4)), dma((chips, 4)), dma((CHUNKS,)), dma((CHUNKS,)),
-            dma((CHUNKS, chips)), dma((CHUNKS, chips)), dma, dma,
+            pltpu.VMEM(table_shape, jnp.int32),
+            pltpu.SMEM(table_shape, jnp.int32),
+            dma, dma((2,)), dma, dma,
+            dma, dma((chips // 2 + 1, 2, 4)),
+            dma, dma((2, 2)),
+            dma, dma((chips,)), dma, dma((CHUNKS,)),
+            dma, dma((CHUNKS,)), dma, dma,
         ],
         compiler_params=pltpu.CompilerParams(
             collective_id=0, has_side_effects=True, vmem_limit_bytes=67043328
         ),
-    )(table, slots, tokens, cotangent, block_weights.reshape(n_slots * n_dp, part, width))
-    weight_grad = jnp.where(live[:, None, None], weight_sum, jnp.zeros((), BF16))
-    return (input_sum.astype(BF16), weight_grad)
+    )(
+        counts, slot_target.reshape(slot_rows), slot_block.reshape(slot_rows), tokens, cotangent,
+        block_weights.reshape(n_slots * n_dp, part, width),
+    )
+    gathers = 8
+    return pl.pallas_call(
+        gather_kernel,
+        out_shape=(
+            jax.ShapeDtypeStruct((rows, features), BF16),
+            jax.ShapeDtypeStruct((n_slots, part, width), BF16),
+        ),
+        in_specs=[smem, smem, smem, vmem, hbm],
+        out_specs=(vmem, hbm),
+        scratch_shapes=[
+            pltpu.VMEM((n_slots, part, width), BF16), dma((gathers,)), dma((gathers,)),
+        ],
+    )(counts, slot_target, slot_block, input_sum, grad_blocks)
 
 
 def solution(mesh):
@@ -518,7 +590,7 @@
 
     def body(*args):
         tokens, weights = args[0], args[2]
-        if paired and tokens.shape[0] % 16 == 0 and weights.shape[0] // SPC % (n_cols // 4) == 0:
+        if paired and tokens.shape[0] % 16 == 0 and weights.shape[0] % LANES == 0 and weights.shape[0] // SPC % (n_cols // 4) == 0:
             return kernel_shards(n_cols, *args)
         return shards(*args)
 

time: 81.5 us -> 78.6 us (0.964)
  the two profiles are of different devices: /device:TPU:0 before, /device:TPU:9 now
where the time goes in v1:
time: 78.6 us; the launch traced here: 77.3 us
  Pallas kernels  76 us (97%)
  between operations  1.29 us (2%)
    pallas_call x1, Pallas kernels, kernel_shards(): pl.pallas_call(functools.partial(layer_kernel, n_cols), out_shape=(jax.Sh...  68.7 us
    pallas_call x1, Pallas kernels, kernel_shards(): pl.pallas_call(gather_kernel, out_shape=(jax.ShapeDtypeStruct((rows, feat...  7.27 us

profile of v1, /device:TPU:9, one launch (start us, length us, event | category | flops | bytes accessed | tf_op | source)
XLA Modules:
  0.0 77.3 jit_solution(2987673588229248049)
XLA Ops:
  1.3 68.7 %shard_map.77 = (f32[16,4096]{1,0:T(8,128)}, bf16[769,64,128]{2,1,0:T(8,128)(2,1)}) custom-call(s32[1]{0:T(128)S(6)} %copy.8.count_ref, s32[2,128]{1,0:T(2,128)} %bitcast.4, s32[2,128]{1,0:T(2,128)} %bitcast.5, bf16[16,4096]{1,0:T(8,128)(2,1)} %tok_ref.1, bf16[16,4096]{1,0:T(8,128)(2,1)} %cot_ref.1, bf16[512,64,128]{2,1,0:T(8,128)(2,1)} %bitcast.3), custom_call_target="tpu_custom_call" | custom-call | tf_op jit(solution)/shard_map/pallas_call | solution.py:531
  70.0 7.3 %shard_map.78 = (bf16[16,4096]{1,0:T(8,128)(2,1)}, bf16[256,64,128]{2,1,0:T(8,128)(2,1)}) custom-call(s32[1]{0:T(128)S(6)} %copy.8.count_ref, s32[256]{0:T(256)} %target_ref.1, s32[256]{0:T(256)} %block_ref.1, f32[16,4096]{1,0:T(8,128)} %get-tuple-element.4.sum_ref, bf16[769,64,128]{2,1,0:T(8,128)(2,1)} %get-tuple-element.5.blocks_ref), custom_call_target="tpu_custom_call" | custom-call | tf_op jit(solution)/shard_map/pallas_call | solution.py:573

commit v2 on v1

--- a/solution.py
+++ b/solution.py
@@ -86,14 +86,15 @@
 NT = (((1,), (1,)), ((), ()))
 CHUNKS = 4
 GROUP = 4
+VMEM_LIMIT = 58720256
 LANES = 128
 
 
 def layer_kernel(
     n_cols, count_ref, target_ref, block_ref, tok_ref, cot_ref, w_ref, in_ref, out_ref,
-    tok, cot, blocks, wgu, wd, grads, hid, pre, acc, sib_out, sib_in, chip_sum, a2a,
+    tok, cot, blocks, wgu, wd, grads, hid, acc, sib_out, sib_in, chip_sum, a2a,
     fin_out, fin_in, lhs, hid_t, table_rows, table_ref,
-    w_sem, own_sem, table_sem, out_sem, ring_send, ring_recv, sib_send, sib_recv,
+    w_sem, own_sem, table_sem, ring_send, ring_recv, sib_send, sib_recv,
     x_send, x_recv, half_send, half_recv, a2a_send, a2a_recv, fin_send, fin_recv,
 ):
     chips = n_cols // 2
@@ -108,6 +109,8 @@
     n_h = hidden // width
     zero_at = blocks.shape[0] - 1
     zero_slot = zero_at
+    table_size = zero_slot // LANES
+    n_slots = out_ref.shape[0]
     half = features // 2
     dp = lax.axis_index("dp")
     col = lax.axis_index("cols")
@@ -233,7 +236,9 @@
     number = lax.broadcasted_iota(jnp.int32, slot_place.shape, 0) * LANES + lax.broadcasted_iota(
         jnp.int32, slot_place.shape, 1
     )
-    slot_place = jnp.where(number < count_ref[0], slot_place, -1)
+    live = number < count_ref[0]
+    slot_place = jnp.where(live, slot_place, -1)
+    table_rows[table_size:, :] = jnp.where(live, slot_place, zero_at)
     lane = lax.broadcasted_iota(jnp.int32, (LANES, LANES), 1)
     in_row = lax.broadcasted_iota(jnp.int32, (LANES, LANES), 0)
     columns = [
@@ -308,8 +313,8 @@
     @pl.loop(0, steps)
     def _(s):
         gate, up = before(0, s)
-        pre[s, 0] = gate
-        pre[s, 1] = up
+        acc[s, :, :span] = gate
+        acc[s, :, span:] = up
         advance(s, 1)
 
     cross_arrival(0)
@@ -319,7 +324,7 @@
 
     @pl.loop(0, steps)
     def _(s):
-        after(0, s, pre[s, 0], pre[s, 1])
+        after(0, s, acc[s, :, :span], acc[s, :, span:])
 
     crossed(2)
     crossed(chips - 2)
@@ -400,16 +405,6 @@
                 hid[g, :, pl.ds(h * width, width)].T
             )
     four = GROUP
-    per_piece = 3 * n_h * four
-    cuts = 4
-
-    def send_out(i, c):
-        at = pl.ds(i * per_piece + c * (per_piece // cuts), per_piece // cuts)
-        return pltpu.make_async_copy(blocks.at[at], out_ref.at[at], out_sem)
-
-    zero_out = pltpu.make_async_copy(blocks.at[zero_at], out_ref.at[zero_at], table_sem)
-    zero_out.start()
-
     @pl.loop(0, n_f // four)
     def _(i):
         at = pl.multiple_of(i * four * width, four * width)
@@ -419,7 +414,6 @@
                 lhs[pl.ds(b * part, part), pl.ds(g * group_rows, group_rows)] = take_part(
                     piece.reshape(group_rows, width).T
                 )
-        base = i * per_piece
         for n in range(2 * n_h // 4):
             cut = slice(n * 4 * width, (n + 1) * 4 * width)
             out = jnp.dot(
@@ -427,18 +421,21 @@
             ).astype(BF16)
             for h in range(4):
                 for b in range(four):
-                    blocks[base + (n * 4 + h) * four + b] = out[
+                    blocks[(n * 4 + h) * n_f + i * four + b] = out[
                         b * part:(b + 1) * part, h * width:(h + 1) * width
                     ]
         c = cot[:, :, :, pl.ds(at, four * width)].reshape(2 * group_rows, four * width)
         out = jnp.dot(hid_t[...], c, preferred_element_type=F32).astype(BF16)
         for h in range(n_h):
             for b in range(four):
-                blocks[base + (2 * n_h + h) * four + b] = out[
+                blocks[(2 * n_h + h) * n_f + i * four + b] = out[
                     h * part:(h + 1) * part, b * width:(b + 1) * width
                 ]
-        for c in range(cuts):
-            send_out(i, c).start()
+
+    for r in range(n_slots // LANES):
+        @pl.loop(0, LANES, unroll=8)
+        def _(j):
+            out_ref[r * LANES + j] = blocks[table_ref[table_size + r, j]]
 
     mine = pl.ds(pl.multiple_of(chip * chip_rows, chip_rows), chip_rows)
 
@@ -451,7 +448,9 @@
         low, high = total[:rows], total[rows:]
         at = pl.multiple_of(i * chunk, chunk)
         fin_out[:, pl.ds(at, chunk)] = jnp.where(core == 0, high, low)
-        in_ref[:, pl.ds(pl.multiple_of(core * half + at, chunk), chunk)] = jnp.where(core == 0, low, high)
+        in_ref[:, pl.ds(pl.multiple_of(core * half + at, chunk), chunk)] = jnp.where(
+            core == 0, low, high
+        ).astype(BF16)
 
     fin = pltpu.make_async_remote_copy(
         src_ref=fin_out, dst_ref=fin_in, send_sem=fin_send, recv_sem=fin_recv,
@@ -464,50 +463,8 @@
     bulk(tok, sib_send, sib_recv.at[0, 0], (dp, sibling)).wait_send()
     bulk(tok.at[0, pl.ds(0, 2 * (chips - 2))], x_send, x_recv.at[0], (1 - dp, col)).wait_send()
     bulk(tok.at[:, pl.ds(0, chips + 1)], ring_send, ring_recv.at[0, 0, 0], (dp, right)).wait_send()
-    zero_out.wait()
-    all_out = pl.ds(0, zero_at)
-    pltpu.make_async_copy(blocks.at[all_out], out_ref.at[all_out], out_sem).wait()
-
     fin.wait()
-    in_ref[:, pl.ds(pl.multiple_of((1 - core) * half, half), half)] = fin_in[...]
-
-
-def gather_kernel(
-    count_ref, target_ref, block_ref, sum_ref, blocks_ref, in_ref, wg_ref, buf, in_sem, out_sem
-):
-    n_slots = wg_ref.shape[0]
-    chunks = in_sem.shape[0]
-    per_chunk = n_slots // chunks
-    zero_at = blocks_ref.shape[0] - 1
-    targets = 3 * (n_slots // SPC)
-    per_piece = targets * GROUP
-    count = count_ref[0]
-
-    @pl.loop(0, chunks)
-    def _(c):
-        for j in range(per_chunk):
-            s = c * per_chunk + j
-            f = block_ref[s]
-            at = (f // GROUP) * per_piece + target_ref[s] * GROUP + f % GROUP
-            pltpu.make_async_copy(
-                blocks_ref.at[jnp.where(s < count, at, zero_at)], buf.at[s], in_sem.at[c]
-            ).start()
-
-    in_ref[...] = sum_ref[...].astype(BF16)
-
-    def out(c):
-        at = pl.ds(c * per_chunk, per_chunk)
-        return pltpu.make_async_copy(buf.at[at], wg_ref.at[at], out_sem.at[c])
-
-    @pl.loop(0, chunks)
-    def _(c):
-        at = pl.ds(c * per_chunk, per_chunk)
-        pltpu.make_async_copy(blocks_ref.at[pl.ds(0, per_chunk)], buf.at[at], in_sem.at[c]).wait()
-        out(c).start()
-
-    @pl.loop(0, chunks)
-    def _(c):
-        out(c).wait()
+    in_ref[:, pl.ds(pl.multiple_of((1 - core) * half, half), half)] = fin_in[...].astype(BF16)
 
 
 def kernel_shards(n_cols, tokens, cotangent, block_weights, slot_block, slot_target, counts):
@@ -526,16 +483,16 @@
     vmem = pl.BlockSpec(memory_space=pltpu.VMEM)
     smem = pl.BlockSpec(memory_space=pltpu.SMEM)
     hbm = pl.BlockSpec(memory_space=pl.ANY)
-    table_shape = (places // LANES, LANES)
+    table_shape = (places // LANES + n_slots // LANES, LANES)
     slot_rows = (n_slots // LANES, LANES)
-    input_sum, grad_blocks = pl.pallas_call(
+    return pl.pallas_call(
         functools.partial(layer_kernel, n_cols),
         out_shape=(
-            jax.ShapeDtypeStruct((rows, features), F32),
-            jax.ShapeDtypeStruct((places + 1, part, width), BF16),
+            pltpu.VMEM((rows, features), BF16),
+            pltpu.VMEM((n_slots, part, width), BF16),
         ),
         in_specs=[smem, vmem, vmem, hbm, hbm, hbm],
-        out_specs=(vmem, hbm),
+        out_specs=(vmem, vmem),
         scratch_shapes=[
             pltpu.VMEM((n_dp, n_cols, rows, features), BF16),
             pltpu.VMEM((n_dp, n_cols, rows, features), BF16),
@@ -544,7 +501,6 @@
             pltpu.VMEM((hidden, features), BF16),
             pltpu.VMEM((n_dp, group_rows, 2 * hidden), BF16),
             pltpu.VMEM((n_dp, group_rows, hidden), BF16),
-            pltpu.VMEM((chips // 2, 2, group_rows, hidden // (chips // 2)), F32),
             pltpu.VMEM((CHUNKS, group_rows, half // CHUNKS), F32),
             pltpu.VMEM((CHUNKS, group_rows, half // CHUNKS), BF16),
             pltpu.VMEM((CHUNKS, group_rows, half // CHUNKS), BF16),
@@ -556,32 +512,19 @@
             pltpu.VMEM((hidden // n_dp, n_dp * group_rows), BF16),
             pltpu.VMEM(table_shape, jnp.int32),
             pltpu.SMEM(table_shape, jnp.int32),
-            dma, dma((2,)), dma, dma,
+            dma, dma((2,)), dma,
             dma, dma((chips // 2 + 1, 2, 4)),
             dma, dma((2, 2)),
             dma, dma((chips,)), dma, dma((CHUNKS,)),
             dma, dma((CHUNKS,)), dma, dma,
         ],
         compiler_params=pltpu.CompilerParams(
-            collective_id=0, has_side_effects=True, vmem_limit_bytes=67043328
+            collective_id=0, has_side_effects=True, vmem_limit_bytes=VMEM_LIMIT
         ),
     )(
         counts, slot_target.reshape(slot_rows), slot_block.reshape(slot_rows), tokens, cotangent,
         block_weights.reshape(n_slots * n_dp, part, width),
     )
-    gathers = 8
-    return pl.pallas_call(
-        gather_kernel,
-        out_shape=(
-            jax.ShapeDtypeStruct((rows, features), BF16),
-            jax.ShapeDtypeStruct((n_slots, part, width), BF16),
-        ),
-        in_specs=[smem, smem, smem, vmem, hbm],
-        out_specs=(vmem, hbm),
-        scratch_shapes=[
-            pltpu.VMEM((n_slots, part, width), BF16), dma((gathers,)), dma((gathers,)),
-        ],
-    )(counts, slot_target, slot_block, input_sum, grad_blocks)
 
 
 def solution(mesh):

time: 78.6 us -> 73.2 us (0.931)
  the two profiles are of different devices: /device:TPU:9 before, /device:TPU:0 now
where the time goes in v2:
time: 73.2 us; the launch traced here: 73 us
  Pallas kernels  69 us (94%)
  local copies, waits for them, and re-layouts  2.67 us (4%)
  between operations  1.29 us (2%)
    pallas_call x1, Pallas kernels, kernel_shards(): pl.pallas_call(functools.partial(layer_kernel, n_cols), out_shape=(pltpu....  69 us
    unnamed x2, local copies, waits for them, and re-layouts  2.67 us

profile of v2, /device:TPU:0, one launch (start us, length us, event | category | flops | bytes accessed | tf_op | source)
XLA Modules:
  0.0 73.0 jit_solution(17955704094685531171)
XLA Ops:
  1.3 69.0 %shard_map.77 = (bf16[16,4096]{1,0:T(8,128)(2,1)S(1)}, bf16[256,64,128]{2,1,0:T(8,128)(2,1)S(1)}) custom-call(s32[1]{0:T(128)S(6)} %copy.12.count_ref, s32[2,128]{1,0:T(2,128)} %bitcast.4, s32[2,128]{1,0:T(2,128)} %bitcast.5, bf16[16,4096]{1,0:T(8,128)(2,1)} %tok_ref.1, bf16[16,4096]{1,0:T(8,128)(2,1)} %cot_ref.1, bf16[512,64,128]{2,1,0:T(8,128)(2,1)} %bitcast.3), custom_call_target="tpu_custom_call" | custom-call | tf_op jit(solution)/shard_map/pallas_call | solution.py:488
  70.3 0.7 copy.10
  71.0 2.0 %copy.11 = bf16[256,64,128]{2,1,0:T(8,128)(2,1)} copy(bf16[256,64,128]{2,1,0:T(8,128)(2,1)S(1)} %get-tuple-element.3) | data formatting | bytes 8388608

commit v3 on v2

--- a/solution.py
+++ b/solution.py
@@ -131,7 +131,6 @@
     for own in owns:
         own.start()
     w_copy = pltpu.make_async_copy(w_ref, blocks.at[pl.ds(0, w_ref.shape[0])], w_sem)
-    w_copy.start()
     barrier = pltpu.get_barrier_semaphore()
     for r in range(1, chips):
         pl.semaphore_signal(barrier, inc=1, device_id=(dp, ((chip + r) % chips) * 2 + core), device_id_type=MESH)
@@ -177,39 +176,35 @@
             device_id=(1 - dp, col), device_id_type=MESH,
         )
 
-    def first(g, arr):
-        for a in (2 * arr, 2 * arr + 1):
-            for direction in range(2):
-                ring(g, direction, 0, a).start()
-        for a in (2 * arr, 2 * arr + 1):
-            share(g, 0, a).start()
-            if g == 0:
-                cross(0, a).start()
-
-    def pass_on(s, direction, a):
-        ring_arrival(0, direction, s, a).wait_recv()
-
-        far = steps - 1 if a % 2 == direction else steps - 2
-
-        @pl.when(s < far)
-        def _():
-            ring(0, direction, s + 1, a).start()
-
-        k = 1 + s if direction == 0 else chips - 1 - s
-        share(0, k, a).start()
-
-        @pl.when(s > 0)
-        def _():
-            cross(k, a).start()
-
-    def advance(s, arr):
+    def piece_of(arr, direction, far):
+        return 2 * arr + (direction if far else 1 - direction)
+
+    def send(g, arr, s, far):
         for direction in range(2):
-            pass_on(s, direction, 2 * arr + direction)
-
-        @pl.when(s < steps - 1)
-        def _():
-            for direction in range(2):
-                pass_on(s, direction, 2 * arr + 1 - direction)
+            ring(g, direction, s, piece_of(arr, direction, far)).start()
+
+    def arrive(arr, s, far, forward):
+        for direction in range(2):
+            a = piece_of(arr, direction, far)
+            ring_arrival(0, direction, s, a).wait_recv()
+            if forward and s < (steps - 1 if far else steps - 2):
+                ring(0, direction, s + 1, a).start()
+            k = 1 + s if direction == 0 else chips - 1 - s
+            share(0, k, a).start()
+            if s > 1 or (s == 1 and not far):
+                cross(k, a).start()
+
+    def passed(s, far):
+        arrive(1, s, far, True)
+
+    def arrive_other(s, far):
+        for direction in range(2):
+            for arr in range(2):
+                a = piece_of(arr, direction, far)
+                ring_arrival(1, direction, s, a).wait_recv()
+                if far and s == 0:
+                    ring(1, direction, 1, a).start()
+                share(1, 1 + s if direction == 0 else chips - 1 - s, a).start()
 
     def bulk(ref, send_sem, recv_sem, device):
         return pltpu.make_async_remote_copy(
@@ -220,17 +215,23 @@
     def all_shared(g, arr):
         bulk(sides[arr][1].at[g, pl.ds(0, chips)], sib_send, sib_recv.at[g, arr], (dp, sibling)).wait_recv()
 
-    def cross_arrival(k):
-        bulk(tok.at[1, pl.ds(0, 2)], x_send, x_recv.at[k], (1 - dp, col)).wait_recv()
-
-    def crossed(k):
-        cross_arrival(k)
-        for a in range(4):
+    def cross_arrival(k, count=2):
+        bulk(tok.at[1, pl.ds(0, count)], x_send, x_recv.at[k], (1 - dp, col)).wait_recv()
+
+    def crossed(k, pieces=range(4)):
+        cross_arrival(k, len(pieces) // 2)
+        for a in pieces:
             share(1, k, a).start()
 
     for own in owns:
         own.wait()
-    first(0, 0)
+    w_copy.start()
+    send(0, 0, 0, True)
+    send(0, 0, 0, False)
+    send(0, 1, 0, True)
+    for a in range(4):
+        cross(0, a).start()
+        share(0, 0, a).start()
 
     slot_place = target_ref[...] * n_f + block_ref[...]
     number = lax.broadcasted_iota(jnp.int32, slot_place.shape, 0) * LANES + lax.broadcasted_iota(
@@ -276,18 +277,20 @@
 
     per_step = n_h // steps
 
-    @pl.loop(0, steps)
-    def _(s):
+    waiting = [(s, far) for s in range(steps) for far in (True, False) if far or s < steps - 1]
+    for s in range(steps):
         @pl.loop(0, n_f)
         def _(f):
             for j in range(per_step):
                 spread(s * per_step + j, f)
 
-        advance(s, 0)
-
-        @pl.when(s == steps // 2 - 1)
-        def _():
-            first(0, 1)
+        arrive(0, s, True, True)
+        if s < steps - 1:
+            arrive(0, s, False, True)
+        if s == 0:
+            send(0, 1, 0, False)
+        for _ in range(min(s, 1) + (s == steps - 1)):
+            passed(*waiting.pop(0))
 
     all_shared(0, 0)
     span = hidden // steps
@@ -310,24 +313,32 @@
         grads[g, :, pl.ds(at, span)] = (back * up * sig * (1.0 + gate * (1.0 - sig))).astype(BF16)
         grads[g, :, pl.ds(pl.multiple_of(hidden + at, span), span)] = (back * silu).astype(BF16)
 
-    @pl.loop(0, steps)
-    def _(s):
+    for s in range(steps):
         gate, up = before(0, s)
         acc[s, :, :span] = gate
         acc[s, :, span:] = up
-        advance(s, 1)
-
-    cross_arrival(0)
-    first(1, 0)
-    first(1, 1)
+        if s < steps - 2:
+            passed(*waiting.pop(0))
+        if s == steps - 3:
+            cross_arrival(0)
+            for far in (True, False):
+                for arr in range(2):
+                    send(1, arr, 0, far)
+            for a in range(4):
+                share(1, 0, a).start()
+
+    while waiting:
+        passed(*waiting.pop(0))
+
     all_shared(0, 1)
 
     @pl.loop(0, steps)
     def _(s):
         after(0, s, acc[s, :, :span], acc[s, :, span:])
 
-    crossed(2)
-    crossed(chips - 2)
+    crossed(2, (1, 3))
+    crossed(chips - 2, (0, 2))
+    arrive_other(0, True)
 
     chunk = half // CHUNKS
     chip_rows = group_rows // chips
@@ -374,14 +385,19 @@
         def _():
             pair_sum(i - 1)
 
+        @pl.when(i == 0)
+        def _():
+            arrive_other(0, False)
+
+        @pl.when(i == CHUNKS - 2)
+        def _():
+            arrive_other(1, True)
+            crossed(3)
+            crossed(chips - 3)
+
     pair_sum(CHUNKS - 1)
 
-    for direction in range(2):
-        for a in range(4):
-            ring_arrival(1, direction, 0, a).wait_recv()
-            share(1, 1 if direction == 0 else chips - 1, a).start()
-
-    @pl.loop(3, chips - 2)
+    @pl.loop(4, chips - 3)
     def _(k):
         crossed(k)
 
@@ -461,8 +477,8 @@
     bulk(sib_out, half_send, half_recv.at[0], (dp, sibling)).wait_send()
     bulk(chip_sum.at[:, pl.ds(1, chips - 1)], a2a_send, a2a_recv.at[0], (dp, sibling)).wait_send()
     bulk(tok, sib_send, sib_recv.at[0, 0], (dp, sibling)).wait_send()
-    bulk(tok.at[0, pl.ds(0, 2 * (chips - 2))], x_send, x_recv.at[0], (1 - dp, col)).wait_send()
-    bulk(tok.at[:, pl.ds(0, chips + 1)], ring_send, ring_recv.at[0, 0, 0], (dp, right)).wait_send()
+    bulk(tok.at[0, pl.ds(0, 2 * chips - 6)], x_send, x_recv.at[0], (1 - dp, col)).wait_send()
+    bulk(tok.at[:, pl.ds(0, chips + 2)], ring_send, ring_recv.at[0, 0, 0], (dp, right)).wait_send()
     fin.wait()
     in_ref[:, pl.ds(pl.multiple_of((1 - core) * half, half), half)] = fin_in[...].astype(BF16)
 
@@ -513,7 +529,7 @@
             pltpu.VMEM(table_shape, jnp.int32),
             pltpu.SMEM(table_shape, jnp.int32),
             dma, dma((2,)), dma,
-            dma, dma((chips // 2 + 1, 2, 4)),
+            dma, dma((chips // 2 + 2, 2, 4)),
             dma, dma((2, 2)),
             dma, dma((chips,)), dma, dma((CHUNKS,)),
             dma, dma((CHUNKS,)), dma, dma,
@@ -529,7 +545,7 @@
 
 def solution(mesh):
     n_dp, n_cols = mesh.shape["dp"], mesh.shape["cols"]
-    paired = n_dp == 2 and n_cols % 4 == 0
+    paired = n_dp == 2 and n_cols % 4 == 0 and n_cols > 12
 
     def body(*args):
         tokens, weights = args[0], args[2]

time: 73.2 us -> 68.9 us (0.941)
  Pallas kernels: 69 us -> 64.8 us
    pallas_call x1, Pallas kernels: 69 us -> 64.8 us  [kernel_shards(): pl.pallas_call(functools.partial(layer_kernel, n_cols), out_shape=(pltpu....]
where the time goes in v3:
time: 68.9 us; the launch traced here: 68.7 us
  Pallas kernels  64.8 us (94%)
  local copies, waits for them, and re-layouts  2.67 us (4%)
  between operations  1.29 us (2%)
    pallas_call x1, Pallas kernels, kernel_shards(): pl.pallas_call(functools.partial(layer_kernel, n_cols), out_shape=(pltpu....  64.8 us
    unnamed x2, local copies, waits for them, and re-layouts  2.67 us

profile of v3, /device:TPU:0, one launch (start us, length us, event | category | flops | bytes accessed | tf_op | source)
XLA Modules:
  0.0 68.7 jit_solution(15049047065229543862)
XLA Ops:
  1.3 64.8 %shard_map.77 = (bf16[16,4096]{1,0:T(8,128)(2,1)S(1)}, bf16[256,64,128]{2,1,0:T(8,128)(2,1)S(1)}) custom-call(s32[1]{0:T(128)S(6)} %copy.12.count_ref, s32[2,128]{1,0:T(2,128)} %bitcast.4, s32[2,128]{1,0:T(2,128)} %bitcast.5, bf16[16,4096]{1,0:T(8,128)(2,1)} %tok_ref.1, bf16[16,4096]{1,0:T(8,128)(2,1)} %cot_ref.1, bf16[512,64,128]{2,1,0:T(8,128)(2,1)} %bitcast.3), custom_call_target="tpu_custom_call" | custom-call | tf_op jit(solution)/shard_map/pallas_call | solution.py:504
  66.1 0.7 copy.10
  66.7 2.0 %copy.11 = bf16[256,64,128]{2,1,0:T(8,128)(2,1)} copy(bf16[256,64,128]{2,1,0:T(8,128)(2,1)S(1)} %get-tuple-element.3) | data formatting | bytes 8388608

commit v4 on v3

--- a/solution.py
+++ b/solution.py
@@ -86,16 +86,18 @@
 NT = (((1,), (1,)), ((), ()))
 CHUNKS = 4
 GROUP = 4
-VMEM_LIMIT = 58720256
+OUT_CUTS = 8
+COPY_LIMIT = 1 << 20
+VMEM_LIMIT = 60817408
 LANES = 128
 
 
 def layer_kernel(
     n_cols, count_ref, target_ref, block_ref, tok_ref, cot_ref, w_ref, in_ref, out_ref,
-    tok, cot, blocks, wgu, wd, grads, hid, acc, sib_out, sib_in, chip_sum, a2a,
-    fin_out, fin_in, lhs, hid_t, table_rows, table_ref,
-    w_sem, own_sem, table_sem, ring_send, ring_recv, sib_send, sib_recv,
-    x_send, x_recv, half_send, half_recv, a2a_send, a2a_recv, fin_send, fin_recv,
+    tok, cot, blocks, wgu, wd, grads, hid, acc, sib_out, sib_in, pair_out, pair_in, line_out, line_in,
+    fin_out, fin_in, lhs, hid_t, slots, table_rows, table_ref,
+    w_sem, own_sem, slot_sem, table_sem, ring_send, ring_recv, sib_send, sib_recv,
+    x_send, x_recv, half_send, half_recv, pair_send, pair_recv, line_send, line_recv, fin_send, fin_recv,
 ):
     chips = n_cols // 2
     steps = chips // 2
@@ -108,8 +110,9 @@
     hidden = wd.shape[0]
     n_h = hidden // width
     zero_at = blocks.shape[0] - 1
-    zero_slot = zero_at
-    table_size = zero_slot // LANES
+    pieces = width // part
+    dead = w_ref.shape[0]
+    table_size = zero_at // LANES
     n_slots = out_ref.shape[0]
     half = features // 2
     dp = lax.axis_index("dp")
@@ -127,6 +130,11 @@
     sibling = chip * 2 + 1 - core
     sides = ((tok_ref, tok), (cot_ref, cot))
 
+    slot_copies = [
+        pltpu.make_async_copy(ref, slots.at[a], slot_sem.at[a]) for a, ref in enumerate((target_ref, block_ref))
+    ]
+    for copy in slot_copies:
+        copy.start()
     owns = [pltpu.make_async_copy(sides[a][0], sides[a][1].at[0, col], own_sem.at[a]) for a in range(2)]
     for own in owns:
         own.start()
@@ -233,11 +241,13 @@
         cross(0, a).start()
         share(0, 0, a).start()
 
-    slot_place = target_ref[...] * n_f + block_ref[...]
+    for copy in slot_copies:
+        copy.wait()
+    slot_place = slots[0] * n_f + slots[1]
     number = lax.broadcasted_iota(jnp.int32, slot_place.shape, 0) * LANES + lax.broadcasted_iota(
         jnp.int32, slot_place.shape, 1
     )
-    live = number < count_ref[0]
+    live = number < count_ref[...]
     slot_place = jnp.where(live, slot_place, -1)
     table_rows[table_size:, :] = jnp.where(live, slot_place, zero_at)
     lane = lax.broadcasted_iota(jnp.int32, (LANES, LANES), 1)
@@ -245,52 +255,54 @@
     columns = [
         jnp.broadcast_to(slot_place[j:j + 1], (LANES, LANES)).T for j in range(slot_place.shape[0])
     ]
-    for t in range(zero_slot // LANES):
+    for t in range(table_size):
         row = jnp.zeros((1, LANES), jnp.int32)
         for j, column in enumerate(columns):
             hit = column == lane + t * LANES
             row = row + jnp.sum(
-                jnp.where(hit, in_row + (j * LANES - zero_slot), 0), axis=0, keepdims=True
+                jnp.where(hit, pieces * (in_row + j * LANES) - dead, 0), axis=0, keepdims=True
             )
-        table_rows[t:t + 1, :] = row + zero_slot
+        table_rows[t:t + 1, :] = row + dead
     table_copy = pltpu.make_async_copy(table_rows, table_ref, table_sem)
     table_copy.start()
-    blocks[zero_at] = jnp.zeros((part, width), BF16)
+    for at in [zero_at] + list(range(dead, dead + pieces)):
+        blocks[at] = jnp.zeros((part, width), BF16)
     w_copy.wait()
     table_copy.wait()
 
-    pieces = width // part
-
     def spread(h, f):
         at = pl.multiple_of(f * width, width)
-        hid_at = pl.multiple_of(h * width, width)
+        hid_at = h * width
         for k in range(3):
-            entry = (k * n_h + h) * n_f + f
-            index = table_ref[entry // LANES, entry % LANES]
+            row, lane = divmod((k * n_h + h) * n_f, LANES)
+            base = table_ref[row, lane + f]
             for piece in range(pieces):
-                value = blocks[jnp.minimum(index * pieces + piece, zero_at)]
+                value = blocks[base + piece]
                 if k < 2:
                     wgu[pl.ds(pl.multiple_of(at + piece * part, part), part),
-                        pl.ds(pl.multiple_of(k * hidden + hid_at, width), width)] = value
+                        pl.ds(k * hidden + hid_at, width)] = value
                 else:
-                    wd[pl.ds(pl.multiple_of(hid_at + piece * part, part), part), pl.ds(at, width)] = value
+                    wd[pl.ds(hid_at + piece * part, part), pl.ds(at, width)] = value
 
     per_step = n_h // steps
 
     waiting = [(s, far) for s in range(steps) for far in (True, False) if far or s < steps - 1]
     for s in range(steps):
-        @pl.loop(0, n_f)
-        def _(f):
-            for j in range(per_step):
-                spread(s * per_step + j, f)
-
+        if s == steps - 1:
+            passed(*waiting.pop(0))
         arrive(0, s, True, True)
         if s < steps - 1:
             arrive(0, s, False, True)
         if s == 0:
             send(0, 1, 0, False)
-        for _ in range(min(s, 1) + (s == steps - 1)):
+        elif s < steps - 1:
             passed(*waiting.pop(0))
+        if s < steps - 1:
+            for u in range(2 * steps * s // (steps - 1), 2 * steps * (s + 1) // (steps - 1)):
+                @pl.loop(u % 2 * n_f // 2, (u % 2 + 1) * n_f // 2, unroll=4)
+                def _(f):
+                    for j in range(per_step):
+                        spread(u // 2 * per_step + j, f)
 
     all_shared(0, 0)
     span = hidden // steps
@@ -317,8 +329,7 @@
         gate, up = before(0, s)
         acc[s, :, :span] = gate
         acc[s, :, span:] = up
-        if s < steps - 2:
-            passed(*waiting.pop(0))
+        passed(*waiting.pop(0))
         if s == steps - 3:
             cross_arrival(0)
             for far in (True, False):
@@ -327,9 +338,6 @@
             for a in range(4):
                 share(1, 0, a).start()
 
-    while waiting:
-        passed(*waiting.pop(0))
-
     all_shared(0, 1)
 
     @pl.loop(0, steps)
@@ -352,27 +360,53 @@
             device_id=(dp, sibling), device_id_type=MESH,
         )
 
-    def spread_sum(r, i):
-        other = (chip + r) % chips
+    lines = chips // 2
+    line, side = chip // 2, chip % 2
+
+    def rows_of(zz, yy):
+        return pl.ds(pl.multiple_of((2 * zz + yy) * chip_rows, chip_rows), chip_rows)
+
+    def to_partner(i):
         return pltpu.make_async_remote_copy(
-            src_ref=chip_sum.at[i, other], dst_ref=a2a.at[i, r],
-            send_sem=a2a_send, recv_sem=a2a_recv.at[i],
-            device_id=(dp, other * 2 + core), device_id_type=MESH,
+            src_ref=pair_out.at[i], dst_ref=pair_in.at[i], send_sem=pair_send, recv_sem=pair_recv.at[i],
+            device_id=(dp, (2 * line + 1 - side) * 2 + core), device_id_type=MESH,
+        )
+
+    def along_line(r, i):
+        other = (line + r) % lines
+        return pltpu.make_async_remote_copy(
+            src_ref=line_out.at[i, other], dst_ref=line_in.at[i, r],
+            send_sem=line_send, recv_sem=line_recv.at[i],
+            device_id=(dp, (2 * other + side) * 2 + core), device_id_type=MESH,
         )
 
     def pair_sum(i):
         to_sibling(i).wait_recv()
 
-        @pl.loop(0, chips)
-        def _(c):
-            at = pl.ds(pl.multiple_of(c * chip_rows, chip_rows), chip_rows)
-            total = acc[i, at, :] + sib_in[i, at, :].astype(F32)
+        @pl.loop(0, lines)
+        def _(zz):
+            at = rows_of(zz, 1 - side)
+            pair_out[i, zz] = (acc[i, at, :] + sib_in[i, at, :].astype(F32)).astype(BF16)
+
+        to_partner(i).start()
+
+        @pl.loop(0, lines)
+        def _(zz):
+            at = rows_of(zz, side)
+            acc[i, at, :] = acc[i, at, :] + sib_in[i, at, :].astype(F32)
+
+    def line_sum(i):
+        to_partner(i).wait_recv()
+
+        @pl.loop(0, lines)
+        def _(zz):
+            at = rows_of(zz, side)
+            total = acc[i, at, :] + pair_in[i, zz].astype(F32)
             acc[i, at, :] = total
-            chip_sum[i, c] = total.astype(BF16)
-
-        @pl.loop(1, chips)
-        def _(r):
-            spread_sum(r, i).start()
+            line_out[i, zz] = total.astype(BF16)
+
+        for r in range(1, lines):
+            along_line(r, i).start()
 
     @pl.loop(0, CHUNKS)
     def _(i):
@@ -389,17 +423,16 @@
         def _():
             arrive_other(0, False)
 
-        @pl.when(i == CHUNKS - 2)
-        def _():
-            arrive_other(1, True)
+        @pl.when(i == CHUNKS - 3)
+        def _():
             crossed(3)
             crossed(chips - 3)
 
-    pair_sum(CHUNKS - 1)
-
-    @pl.loop(4, chips - 3)
-    def _(k):
-        crossed(k)
+        @pl.when(i == CHUNKS - 2)
+        def _():
+            arrive_other(1, True)
+            for k in range(4, chips - 3):
+                crossed(k)
 
     all_shared(1, 0)
     all_shared(1, 1)
@@ -408,6 +441,15 @@
     def _(s):
         gate, up = before(1, s)
         after(1, s, gate, up)
+
+        @pl.when(s == 0)
+        def _():
+            pair_sum(CHUNKS - 1)
+            line_sum(0)
+
+        @pl.when(s >= 2)
+        def _():
+            line_sum(s - 1)
 
     def take_part(block):
         out = block[:part]
@@ -421,66 +463,102 @@
                 hid[g, :, pl.ds(h * width, width)].T
             )
     four = GROUP
-    @pl.loop(0, n_f // four)
-    def _(i):
-        at = pl.multiple_of(i * four * width, four * width)
+    mine = rows_of(line, side)
+    fin = pltpu.make_async_remote_copy(
+        src_ref=fin_out, dst_ref=fin_in, send_sem=fin_send, recv_sem=fin_recv,
+        device_id=(dp, sibling), device_id_type=MESH,
+    )
+
+    def final_sum(i):
+        total = acc[i, mine, :]
+        bulk(line_in.at[i, pl.ds(1, lines - 1)], line_send, line_recv.at[i], (dp, sibling)).wait_recv()
+        for r in range(1, lines):
+            total = total + line_in[i, r].astype(F32)
+        low, high = total[:rows], total[rows:]
+        at = pl.multiple_of(i * chunk, chunk)
+        fin_out[:, pl.ds(at, chunk)] = jnp.where(core == 0, high, low)
+        in_ref[:, pl.ds(pl.multiple_of(core * half + at, chunk), chunk)] = jnp.where(
+            core == 0, low, high
+        ).astype(BF16)
+
+    tiles = n_f // four
+
+    def prepare(i, slot):
+        at = jnp.minimum(i, tiles - 1) * four * width
         for g in range(2):
             for b in range(four):
                 piece = tok[g, :, :, pl.ds(pl.multiple_of(at + b * width, width), width)]
-                lhs[pl.ds(b * part, part), pl.ds(g * group_rows, group_rows)] = take_part(
+                lhs[slot, pl.ds(b * part, part), pl.ds(g * group_rows, group_rows)] = take_part(
                     piece.reshape(group_rows, width).T
                 )
+
+    def tile_grads(i, slot):
         for n in range(2 * n_h // 4):
             cut = slice(n * 4 * width, (n + 1) * 4 * width)
             out = jnp.dot(
-                lhs[...], grads[:, :, cut].reshape(2 * group_rows, 4 * width), preferred_element_type=F32
+                lhs[slot], grads[:, :, cut].reshape(2 * group_rows, 4 * width), preferred_element_type=F32
             ).astype(BF16)
             for h in range(4):
                 for b in range(four):
                     blocks[(n * 4 + h) * n_f + i * four + b] = out[
                         b * part:(b + 1) * part, h * width:(h + 1) * width
                     ]
-        c = cot[:, :, :, pl.ds(at, four * width)].reshape(2 * group_rows, four * width)
-        out = jnp.dot(hid_t[...], c, preferred_element_type=F32).astype(BF16)
+            if n == 0:
+                prepare(i + 1, 1 - slot)
+        c = cot[:, :, :, pl.ds(pl.multiple_of(i * four * width, width), four * width)]
+        out = jnp.dot(
+            hid_t[...], c.reshape(2 * group_rows, four * width), preferred_element_type=F32
+        ).astype(BF16)
         for h in range(n_h):
             for b in range(four):
                 blocks[(2 * n_h + h) * n_f + i * four + b] = out[
                     h * part:(h + 1) * part, b * width:(b + 1) * width
                 ]
 
+    prepare(0, 0)
+
+    @pl.loop(0, tiles // 2)
+    def _(p):
+        tile_grads(2 * p, 0)
+
+        @pl.when(p == 0)
+        def _():
+            line_sum(CHUNKS - 1)
+
+        @pl.when(p == tiles // 2 - 1)
+        def _():
+            @pl.loop(0, CHUNKS)
+            def _(n):
+                final_sum(n)
+
+            fin.start()
+
+        tile_grads(2 * p + 1, 1)
+
     for r in range(n_slots // LANES):
         @pl.loop(0, LANES, unroll=8)
         def _(j):
             out_ref[r * LANES + j] = blocks[table_ref[table_size + r, j]]
 
-    mine = pl.ds(pl.multiple_of(chip * chip_rows, chip_rows), chip_rows)
-
-    @pl.loop(0, CHUNKS)
-    def _(i):
-        total = acc[i, mine, :]
-        bulk(a2a.at[i, pl.ds(1, chips - 1)], a2a_send, a2a_recv.at[i], (dp, sibling)).wait_recv()
-        for r in range(1, chips):
-            total = total + a2a[i, r].astype(F32)
-        low, high = total[:rows], total[rows:]
-        at = pl.multiple_of(i * chunk, chunk)
-        fin_out[:, pl.ds(at, chunk)] = jnp.where(core == 0, high, low)
-        in_ref[:, pl.ds(pl.multiple_of(core * half + at, chunk), chunk)] = jnp.where(
-            core == 0, low, high
-        ).astype(BF16)
-
-    fin = pltpu.make_async_remote_copy(
-        src_ref=fin_out, dst_ref=fin_in, send_sem=fin_send, recv_sem=fin_recv,
-        device_id=(dp, sibling), device_id_type=MESH,
-    )
-    fin.start()
-
     bulk(sib_out, half_send, half_recv.at[0], (dp, sibling)).wait_send()
-    bulk(chip_sum.at[:, pl.ds(1, chips - 1)], a2a_send, a2a_recv.at[0], (dp, sibling)).wait_send()
+    bulk(pair_out, pair_send, pair_recv.at[0], (dp, sibling)).wait_send()
+    bulk(line_out.at[:, pl.ds(1, lines - 1)], line_send, line_recv.at[0], (dp, sibling)).wait_send()
     bulk(tok, sib_send, sib_recv.at[0, 0], (dp, sibling)).wait_send()
     bulk(tok.at[0, pl.ds(0, 2 * chips - 6)], x_send, x_recv.at[0], (1 - dp, col)).wait_send()
     bulk(tok.at[:, pl.ds(0, chips + 2)], ring_send, ring_recv.at[0, 0, 0], (dp, right)).wait_send()
     fin.wait()
     in_ref[:, pl.ds(pl.multiple_of((1 - core) * half, half), half)] = fin_in[...].astype(BF16)
+
+
+def out_kernel(in_ref, wg_ref, in_out, wg_out, in_sem, wg_sem):
+    per_cut = wg_ref.shape[0] // OUT_CUTS
+    first = pltpu.make_async_copy(in_ref, in_out, in_sem)
+    first.start()
+    for c in range(OUT_CUTS):
+        at = pl.ds(c * per_cut, per_cut)
+        pltpu.make_async_copy(wg_ref.at[at], wg_out.at[at], wg_sem).start()
+    first.wait()
+    pltpu.make_async_copy(wg_ref, wg_out, wg_sem).wait()
 
 
 def kernel_shards(n_cols, tokens, cotangent, block_weights, slot_block, slot_target, counts):
@@ -497,17 +575,16 @@
     half = features // 2
     dma = pltpu.SemaphoreType.DMA
     vmem = pl.BlockSpec(memory_space=pltpu.VMEM)
-    smem = pl.BlockSpec(memory_space=pltpu.SMEM)
     hbm = pl.BlockSpec(memory_space=pl.ANY)
     table_shape = (places // LANES + n_slots // LANES, LANES)
     slot_rows = (n_slots // LANES, LANES)
-    return pl.pallas_call(
+    results = pl.pallas_call(
         functools.partial(layer_kernel, n_cols),
         out_shape=(
             pltpu.VMEM((rows, features), BF16),
             pltpu.VMEM((n_slots, part, width), BF16),
         ),
-        in_specs=[smem, vmem, vmem, hbm, hbm, hbm],
+        in_specs=[vmem, hbm, hbm, hbm, hbm, hbm],
         out_specs=(vmem, vmem),
         scratch_shapes=[
             pltpu.VMEM((n_dp, n_cols, rows, features), BF16),
@@ -520,36 +597,50 @@
             pltpu.VMEM((CHUNKS, group_rows, half // CHUNKS), F32),
             pltpu.VMEM((CHUNKS, group_rows, half // CHUNKS), BF16),
             pltpu.VMEM((CHUNKS, group_rows, half // CHUNKS), BF16),
-            pltpu.VMEM((CHUNKS, chips, group_rows // chips, half // CHUNKS), BF16),
-            pltpu.VMEM((CHUNKS, chips, group_rows // chips, half // CHUNKS), BF16),
+            pltpu.VMEM((CHUNKS, chips // 2, group_rows // chips, half // CHUNKS), BF16),
+            pltpu.VMEM((CHUNKS, chips // 2, group_rows // chips, half // CHUNKS), BF16),
+            pltpu.VMEM((CHUNKS, chips // 2, group_rows // chips, half // CHUNKS), BF16),
+            pltpu.VMEM((CHUNKS, chips // 2, group_rows // chips, half // CHUNKS), BF16),
             pltpu.VMEM((rows, half), F32),
             pltpu.VMEM((rows, half), F32),
-            pltpu.VMEM((4 * part, n_dp * group_rows), BF16),
+            pltpu.VMEM((2, GROUP * part, n_dp * group_rows), BF16),
             pltpu.VMEM((hidden // n_dp, n_dp * group_rows), BF16),
+            pltpu.VMEM((2,) + slot_rows, jnp.int32),
             pltpu.VMEM(table_shape, jnp.int32),
             pltpu.SMEM(table_shape, jnp.int32),
-            dma, dma((2,)), dma,
+            dma, dma((2,)), dma((2,)), dma,
             dma, dma((chips // 2 + 2, 2, 4)),
             dma, dma((2, 2)),
             dma, dma((chips,)), dma, dma((CHUNKS,)),
-            dma, dma((CHUNKS,)), dma, dma,
+            dma, dma((CHUNKS,)), dma, dma((CHUNKS,)), dma, dma,
         ],
         compiler_params=pltpu.CompilerParams(
             collective_id=0, has_side_effects=True, vmem_limit_bytes=VMEM_LIMIT
         ),
     )(
-        counts, slot_target.reshape(slot_rows), slot_block.reshape(slot_rows), tokens, cotangent,
+        counts.reshape(1, 1), slot_target.reshape(slot_rows), slot_block.reshape(slot_rows), tokens, cotangent,
         block_weights.reshape(n_slots * n_dp, part, width),
     )
+    return pl.pallas_call(
+        out_kernel,
+        out_shape=(
+            jax.ShapeDtypeStruct((rows, features), BF16),
+            jax.ShapeDtypeStruct((n_slots, part, width), BF16),
+        ),
+        in_specs=[vmem, vmem],
+        out_specs=(hbm, hbm),
+        scratch_shapes=[dma, dma],
+        compiler_params=pltpu.CompilerParams(vmem_limit_bytes=COPY_LIMIT),
+    )(*results)
 
 
 def solution(mesh):
     n_dp, n_cols = mesh.shape["dp"], mesh.shape["cols"]
-    paired = n_dp == 2 and n_cols % 4 == 0 and n_cols > 12
+    paired = n_dp == 2 and n_cols == 4 * CHUNKS
 
     def body(*args):
         tokens, weights = args[0], args[2]
-        if paired and tokens.shape[0] % 16 == 0 and weights.shape[0] % LANES == 0 and weights.shape[0] // SPC % (n_cols // 4) == 0:
+        if paired and tokens.shape[0] % 16 == 0 and weights.shape[0] % LANES == 0 and LANES * weights.shape[1] % tokens.shape[1] == 0 and weights.shape[0] // SPC % (n_cols // 4) == 0:
             return kernel_shards(n_cols, *args)
         return shards(*args)
 

time: 68.9 us -> 63.2 us (0.917)
  Pallas kernels: 64.8 us -> 61.7 us
  local copies, waits for them, and re-layouts: 2.67 us -> 0 us
    pallas_call x1, Pallas kernels: 64.8 us -> 59.7 us  [kernel_shards(): pl.pallas_call(functools.partial(layer_kernel, n_cols), out_shape=(pltpu....]
    unnamed x2 -> x0, local copies, waits for them, and re-layouts: 2.67 us -> none
    pallas_call x0 -> x1, Pallas kernels: none -> 2.06 us  [kernel_shards(): pl.pallas_call(out_kernel, out_shape=(jax.ShapeDtypeStruct((rows, feature...]
where the time goes in v4:
time: 63.2 us; the launch traced here: 63 us
  Pallas kernels  61.7 us (98%)
  between operations  1.29 us (2%)
    pallas_call x1, Pallas kernels, kernel_shards(): pl.pallas_call(functools.partial(layer_kernel, n_cols), out_shape=(pltpu....  59.7 us
    pallas_call x1, Pallas kernels, kernel_shards(): pl.pallas_call(out_kernel, out_shape=(jax.ShapeDtypeStruct((rows, feature...  2.06 us

profile of v4, /device:TPU:0, one launch (start us, length us, event | category | flops | bytes accessed | tf_op | source)
XLA Modules:
  0.0 63.0 jit_solution(3090224591049149928)
XLA Ops:
  1.3 59.7 %shard_map.77 = (bf16[16,4096]{1,0:T(8,128)(2,1)S(1)}, bf16[256,64,128]{2,1,0:T(8,128)(2,1)S(1)}) custom-call(s32[1,1]{1,0:T(1,128)} %bitcast.4.count_ref, s32[2,128]{1,0:T(2,128)} %bitcast.6, s32[2,128]{1,0:T(2,128)} %bitcast.7, bf16[16,4096]{1,0:T(8,128)(2,1)} %tok_ref.1, bf16[16,4096]{1,0:T(8,128)(2,1)} %cot_ref.1, bf16[512,64,128]{2,1,0:T(8,128)(2,1)} %bitcast.5), custom_call_target="tpu_custom_call" | custom-call | tf_op jit(solution)/shard_map/pallas_call | solution.py:581
  61.0 2.1 %shard_map.78 = (bf16[16,4096]{1,0:T(8,128)(2,1)}, bf16[256,64,128]{2,1,0:T(8,128)(2,1)}) custom-call(bf16[16,4096]{1,0:T(8,128)(2,1)S(1)} %get-tuple-element.4.in_ref, bf16[256,64,128]{2,1,0:T(8,128)(2,1)S(1)} %get-tuple-element.5.wg_ref), custom_call_target="tpu_custom_call" | custom-call | tf_op jit(solution)/shard_map/pallas_call | solution.py:624

commit v5 on v4

--- a/solution.py
+++ b/solution.py
@@ -325,10 +325,25 @@
         grads[g, :, pl.ds(at, span)] = (back * up * sig * (1.0 + gate * (1.0 - sig))).astype(BF16)
         grads[g, :, pl.ds(pl.multiple_of(hidden + at, span), span)] = (back * silu).astype(BF16)
 
+    def take_part(block):
+        out = block[:part]
+        for i in range(1, width // part):
+            out = jnp.where(dp == i, block[i * part:(i + 1) * part], out)
+        return out
+
+    def turn_hidden(g):
+        for h in range(n_h):
+            hid_t[pl.ds(h * part, part), pl.ds(g * group_rows, group_rows)] = take_part(
+                hid[g, :, pl.ds(h * width, width)].T
+            )
+
     for s in range(steps):
         gate, up = before(0, s)
-        acc[s, :, :span] = gate
-        acc[s, :, span:] = up
+        sig = jax.nn.sigmoid(gate)
+        silu = gate * sig
+        hid[0, :, s * span:(s + 1) * span] = (silu * up).astype(BF16)
+        acc[s, :, :span] = up * sig * (1.0 + gate * (1.0 - sig))
+        acc[s, :, span:] = silu
         passed(*waiting.pop(0))
         if s == steps - 3:
             cross_arrival(0)
@@ -338,11 +353,16 @@
             for a in range(4):
                 share(1, 0, a).start()
 
+    turn_hidden(0)
     all_shared(0, 1)
 
-    @pl.loop(0, steps)
-    def _(s):
-        after(0, s, acc[s, :, :span], acc[s, :, span:])
+    for s in range(steps):
+        at = s * span
+        back = lax.dot_general(
+            cot[0].reshape(group_rows, features), wd[at:at + span, :], NT, preferred_element_type=F32
+        )
+        grads[0, :, at:at + span] = (back * acc[s, :, :span]).astype(BF16)
+        grads[0, :, hidden + at:hidden + at + span] = (back * acc[s, :, span:]).astype(BF16)
 
     crossed(2, (1, 3))
     crossed(chips - 2, (0, 2))
@@ -380,20 +400,18 @@
             device_id=(dp, (2 * other + side) * 2 + core), device_id_type=MESH,
         )
 
+    def pair_add(i):
+        for zz in range(lines):
+            at = rows_of(zz, 1 - side)
+            pair_out[i, zz] = (acc[i, at, :] + sib_in[i, at, :].astype(F32)).astype(BF16)
+        to_partner(i).start()
+        for zz in range(lines):
+            at = rows_of(zz, side)
+            acc[i, at, :] = acc[i, at, :] + sib_in[i, at, :].astype(F32)
+
     def pair_sum(i):
         to_sibling(i).wait_recv()
-
-        @pl.loop(0, lines)
-        def _(zz):
-            at = rows_of(zz, 1 - side)
-            pair_out[i, zz] = (acc[i, at, :] + sib_in[i, at, :].astype(F32)).astype(BF16)
-
-        to_partner(i).start()
-
-        @pl.loop(0, lines)
-        def _(zz):
-            at = rows_of(zz, side)
-            acc[i, at, :] = acc[i, at, :] + sib_in[i, at, :].astype(F32)
+        pair_add(i)
 
     def line_sum(i):
         to_partner(i).wait_recv()
@@ -408,31 +426,24 @@
         for r in range(1, lines):
             along_line(r, i).start()
 
-    @pl.loop(0, CHUNKS)
-    def _(i):
-        at = pl.multiple_of(i * chunk, chunk)
+    for i in range(CHUNKS):
+        at = i * chunk
         sib_out[i] = terms(pl.multiple_of((1 - core) * half + at, chunk)).astype(BF16)
         to_sibling(i).start()
-        acc[i] = terms(pl.multiple_of(core * half + at, chunk))
-
-        @pl.when(i > 0)
-        def _():
-            pair_sum(i - 1)
-
-        @pl.when(i == 0)
-        def _():
-            arrive_other(0, False)
-
-        @pl.when(i == CHUNKS - 3)
-        def _():
-            crossed(3)
-            crossed(chips - 3)
-
-        @pl.when(i == CHUNKS - 2)
-        def _():
+        if i > 0:
+            to_sibling(i - 1).wait_recv()
+        if i == CHUNKS - 1:
             arrive_other(1, True)
             for k in range(4, chips - 3):
                 crossed(k)
+        acc[i] = terms(pl.multiple_of(core * half + at, chunk))
+        if i > 0:
+            pair_add(i - 1)
+        if i == 0:
+            arrive_other(0, False)
+        if i == CHUNKS - 2:
+            crossed(3)
+            crossed(chips - 3)
 
     all_shared(1, 0)
     all_shared(1, 1)
@@ -451,17 +462,7 @@
         def _():
             line_sum(s - 1)
 
-    def take_part(block):
-        out = block[:part]
-        for i in range(1, width // part):
-            out = jnp.where(dp == i, block[i * part:(i + 1) * part], out)
-        return out
-
-    for g in range(2):
-        for h in range(n_h):
-            hid_t[pl.ds(h * part, part), pl.ds(g * group_rows, group_rows)] = take_part(
-                hid[g, :, pl.ds(h * width, width)].T
-            )
+    turn_hidden(1)
     four = GROUP
     mine = rows_of(line, side)
     fin = pltpu.make_async_remote_copy(
@@ -536,7 +537,7 @@
         tile_grads(2 * p + 1, 1)
 
     for r in range(n_slots // LANES):
-        @pl.loop(0, LANES, unroll=8)
+        @pl.loop(0, LANES, unroll=32)
         def _(j):
             out_ref[r * LANES + j] = blocks[table_ref[table_size + r, j]]
 

time: 63.2 us -> 63.4 us (level)
  no operation moved by 1% of the time
where the time goes in v5:
time: 63.4 us; the launch traced here: 63.2 us
  Pallas kernels  61.8 us (97%)
  between operations  1.45 us (2%)
    pallas_call x1, Pallas kernels, kernel_shards(): pl.pallas_call(functools.partial(layer_kernel, n_cols), out_shape=(pltpu....  59.7 us
    pallas_call x1, Pallas kernels, kernel_shards(): pl.pallas_call(out_kernel, out_shape=(jax.ShapeDtypeStruct((rows, feature...  2.06 us

profile of v5, /device:TPU:0, one launch (start us, length us, event | category | flops | bytes accessed | tf_op | source)
XLA Modules:
  0.0 63.2 jit_solution(1503525495727516020)
XLA Ops:
  1.3 59.7 %shard_map.77 = (bf16[16,4096]{1,0:T(8,128)(2,1)S(1)}, bf16[256,64,128]{2,1,0:T(8,128)(2,1)S(1)}) custom-call(s32[1,1]{1,0:T(1,128)} %bitcast.4.count_ref, s32[2,128]{1,0:T(2,128)} %bitcast.6, s32[2,128]{1,0:T(2,128)} %bitcast.7, bf16[16,4096]{1,0:T(8,128)(2,1)} %tok_ref.1, bf16[16,4096]{1,0:T(8,128)(2,1)} %cot_ref.1, bf16[512,64,128]{2,1,0:T(8,128)(2,1)} %bitcast.5), custom_call_target="tpu_custom_call" | custom-call | tf_op jit(solution)/shard_map/pallas_call | solution.py:582
  61.0 2.1 %shard_map.78 = (bf16[16,4096]{1,0:T(8,128)(2,1)}, bf16[256,64,128]{2,1,0:T(8,128)(2,1)}) custom-call(bf16[16,4096]{1,0:T(8,128)(2,1)S(1)} %get-tuple-element.4.in_ref, bf16[256,64,128]{2,1,0:T(8,128)(2,1)S(1)} %get-tuple-element.5.wg_ref), custom_call_target="tpu_custom_call" | custom-call | tf_op jit(solution)/shard_map/pallas_call | solution.py:625

commit v6 on v5

--- a/solution.py
+++ b/solution.py
@@ -432,18 +432,18 @@
         to_sibling(i).start()
         if i > 0:
             to_sibling(i - 1).wait_recv()
-        if i == CHUNKS - 1:
-            arrive_other(1, True)
-            for k in range(4, chips - 3):
-                crossed(k)
         acc[i] = terms(pl.multiple_of(core * half + at, chunk))
         if i > 0:
             pair_add(i - 1)
         if i == 0:
             arrive_other(0, False)
-        if i == CHUNKS - 2:
+        if i == CHUNKS - 3:
             crossed(3)
             crossed(chips - 3)
+        if i == CHUNKS - 2:
+            arrive_other(1, True)
+            for k in range(4, chips - 3):
+                crossed(k)
 
     all_shared(1, 0)
     all_shared(1, 1)
@@ -456,19 +456,23 @@
         @pl.when(s == 0)
         def _():
             pair_sum(CHUNKS - 1)
-            line_sum(0)
-
-        @pl.when(s >= 2)
+
+        @pl.when(s != CHUNKS - 2)
         def _():
-            line_sum(s - 1)
+            line_sum(jnp.minimum(s, CHUNKS - 2))
 
     turn_hidden(1)
     four = GROUP
     mine = rows_of(line, side)
-    fin = pltpu.make_async_remote_copy(
-        src_ref=fin_out, dst_ref=fin_in, send_sem=fin_send, recv_sem=fin_recv,
-        device_id=(dp, sibling), device_id_type=MESH,
-    )
+    early = half - chunk
+
+    def fin(j):
+        at = pl.ds(0, early) if j == 0 else pl.ds(early, chunk)
+        return pltpu.make_async_remote_copy(
+            src_ref=fin_out.at[:, at], dst_ref=fin_in.at[:, at],
+            send_sem=fin_send.at[j], recv_sem=fin_recv.at[j],
+            device_id=(dp, sibling), device_id_type=MESH,
+        )
 
     def final_sum(i):
         total = acc[i, mine, :]
@@ -528,13 +532,16 @@
 
         @pl.when(p == tiles // 2 - 1)
         def _():
-            @pl.loop(0, CHUNKS)
+            @pl.loop(0, CHUNKS - 1)
             def _(n):
                 final_sum(n)
 
-            fin.start()
+            fin(0).start()
 
         tile_grads(2 * p + 1, 1)
+
+    final_sum(CHUNKS - 1)
+    fin(1).start()
 
     for r in range(n_slots // LANES):
         @pl.loop(0, LANES, unroll=32)
@@ -547,7 +554,8 @@
     bulk(tok, sib_send, sib_recv.at[0, 0], (dp, sibling)).wait_send()
     bulk(tok.at[0, pl.ds(0, 2 * chips - 6)], x_send, x_recv.at[0], (1 - dp, col)).wait_send()
     bulk(tok.at[:, pl.ds(0, chips + 2)], ring_send, ring_recv.at[0, 0, 0], (dp, right)).wait_send()
-    fin.wait()
+    for j in range(2):
+        fin(j).wait()
     in_ref[:, pl.ds(pl.multiple_of((1 - core) * half, half), half)] = fin_in[...].astype(BF16)
 
 
@@ -613,7 +621,7 @@
             dma, dma((chips // 2 + 2, 2, 4)),
             dma, dma((2, 2)),
             dma, dma((chips,)), dma, dma((CHUNKS,)),
-            dma, dma((CHUNKS,)), dma, dma((CHUNKS,)), dma, dma,
+            dma, dma((CHUNKS,)), dma, dma((CHUNKS,)), dma((2,)), dma((2,)),
         ],
         compiler_params=pltpu.CompilerParams(
             collective_id=0, has_side_effects=True, vmem_limit_bytes=VMEM_LIMIT

time: 63.4 us -> 62.4 us (0.984)
  Pallas kernels: 61.8 us -> 60.8 us
    pallas_call x1, Pallas kernels: 59.7 us -> 58.7 us  [kernel_shards(): pl.pallas_call(functools.partial(layer_kernel, n_cols), out_shape=(pltpu....]
where the time goes in v6:
time: 62.4 us; the launch traced here: 62.3 us
  Pallas kernels  60.8 us (97%)
  between operations  1.45 us (2%)
    pallas_call x1, Pallas kernels, kernel_shards(): pl.pallas_call(functools.partial(layer_kernel, n_cols), out_shape=(pltpu....  58.7 us
    pallas_call x1, Pallas kernels, kernel_shards(): pl.pallas_call(out_kernel, out_shape=(jax.ShapeDtypeStruct((rows, feature...  2.06 us

profile of v6, /device:TPU:0, one launch (start us, length us, event | category | flops | bytes accessed | tf_op | source)
XLA Modules:
  0.0 62.3 jit_solution(12636261732385918180)
XLA Ops:
  1.3 58.7 %shard_map.77 = (bf16[16,4096]{1,0:T(8,128)(2,1)S(1)}, bf16[256,64,128]{2,1,0:T(8,128)(2,1)S(1)}) custom-call(s32[1,1]{1,0:T(1,128)} %bitcast.4.count_ref, s32[2,128]{1,0:T(2,128)} %bitcast.6, s32[2,128]{1,0:T(2,128)} %bitcast.7, bf16[16,4096]{1,0:T(8,128)(2,1)} %tok_ref.1, bf16[16,4096]{1,0:T(8,128)(2,1)} %cot_ref.1, bf16[512,64,128]{2,1,0:T(8,128)(2,1)} %bitcast.5), custom_call_target="tpu_custom_call" | custom-call | tf_op jit(solution)/shard_map/pallas_call | solution.py:590
  60.0 2.1 %shard_map.78 = (bf16[16,4096]{1,0:T(8,128)(2,1)}, bf16[256,64,128]{2,1,0:T(8,128)(2,1)}) custom-call(bf16[16,4096]{1,0:T(8,128)(2,1)S(1)} %get-tuple-element.4.in_ref, bf16[256,64,128]{2,1,0:T(8,128)(2,1)S(1)} %get-tuple-element.5.wg_ref), custom_call_target="tpu_custom_call" | custom-call | tf_op jit(solution)/shard_map/pallas_call | solution.py:633
